TPU v7x, 32 devices: a whole 2x2x4 slice. The times are simulated.
32 devices in a mesh: row: 4 (over y, x), col: 8 (over z, core).
Axes of the slice: x: 2, y: 2, z: 4, core: 2. Of those that a mesh axis runs over, the one named last changes fastest.
Arguments:
- velocities: bfloat16 [1024, 30720], P(None, 'row'), may hold values from -60 to 60, as said below
- modes_panel: bfloat16 [30720, 4096], P('row', 'col'), may hold values from -1 to 1
- atom_slot: int32 [10240], P('row'), may hold values from 0 to 2559, as said below
- lag_offsets: int32 [8], replicated, may hold values from 0 to 256, as said below
Outputs:
- correlations: float32 [8, 4096, 4096], P(None, 'row', 'col')
Inputs may be any that keep to these rules, and one draw needn't show every extreme that they name: `velocities`: every snapshot row has its own scale. Within each aligned block of 2560 atoms, atom_slot is a permutation of 0 to 2559. `lag_offsets`: one of the lags equals 256.
All inputs are finite; a program needn't handle non-finite values.
Results may differ from a plain program's by a relative error of at most 0.0041.
Values may be sent and summed in bfloat16 or wider, within the bound.
No kernel may reach another device: no remote copies, remote signals or barrier semaphores. Data moves between devices by JAX's collectives and lax.ppermute only.
A program may use at most 128 MiB of HBM per device.

v0:
```python
import jax
import jax.numpy as jnp
from jax import lax
from jax.sharding import PartitionSpec as P

M = 4096
LAGS = 8
MAXLAG = 256


epsilon = 1e-06


def from_root(block, axis, owner):
    block = jnp.where(lax.axis_index(axis) == owner, block, jnp.zeros_like(block))
    return lax.psum(block, axis)


def reorder(modes_panel, atom_slot):
    per_atom = modes_panel.reshape(atom_slot.shape[0], 3, modes_panel.shape[1])
    return jnp.take(per_atom, atom_slot, axis=0).reshape(modes_panel.shape)


def correlate(row_modes, column_modes, lag_offsets):
    snapshots = column_modes.shape[0]
    padded = jnp.concatenate(
        [column_modes, jnp.zeros((MAXLAG, column_modes.shape[1]), jnp.bfloat16)], axis=0
    )
    results = []
    for number in range(LAGS):
        offset = lag_offsets[number]
        shifted = lax.dynamic_slice_in_dim(padded, offset, snapshots, 0)
        product = lax.dot_general(
            row_modes, shifted, (((0,), (0,)), ((), ())), preferred_element_type=jnp.float32
        )
        results.append(product * lax.rsqrt((snapshots - offset).astype(jnp.float32)))
    return jnp.stack(results)


def local(velocities, modes_panel, atom_slot, lag_offsets):
    panel = reorder(modes_panel, atom_slot)
    row_count = lax.axis_size("row")
    col_count = lax.axis_size("col")
    partial_terms = jnp.dot(velocities, panel, preferred_element_type=jnp.float32)
    projected = lax.psum(partial_terms, "row")
    energy = lax.psum(jnp.sum(projected * projected, axis=1), "col")
    column_modes = (projected * lax.rsqrt(energy / M + epsilon)[:, None]).astype(jnp.bfloat16)
    owners = col_count // row_count
    pieces = [
        from_root(column_modes, "col", lax.axis_index("row") * owners + owner)
        for owner in range(owners)
    ]
    row_modes = jnp.concatenate(pieces, axis=1)
    return correlate(row_modes, column_modes, lag_offsets)


def solution(mesh):
    return jax.shard_map(
        local,
        mesh=mesh,
        in_specs=(P(None, "row"), P("row", "col"), P("row"), P()),
        out_specs=P(None, "row", "col"),
        check_vma=False,
    )
```

profile of v0, /device:TPU:0, one launch (start us, length us, event | category | flops | bytes accessed | tf_op | source)
XLA Modules:
  0.0 267.6 jit_solution(14538257471376262001)
XLA Ops:
  6.5 0.0 all-reduce.5.cloned.1.call-start
  6.5 0.7 compare_select_fusion
  7.2 0.7 compare_and_fusion
  8.0 20.7 %reshape.12 = bf16[2560,3,512]{2,1,0:T(4,128)(2,1)} reshape(bf16[7680,512]{1,0:T(8,128)(2,1)} %param.5) | data formatting | bytes 15728640 | tf_op jit(solution)/shard_map/reshape | solution.py:20
  28.7 17.1 %gather_fusion = bf16[2560,3,512]{2,1,0:T(4,128)(2,1)} fusion(bf16[2560,3,512]{2,1,0:T(4,128)(2,1)} %reshape.12, s32[3072]{0:T(1024)S(1)} %pad_clamp_fusion), kind=kCustom, calls=%fused_computation | custom fusion | bytes 15738880 | tf_op jit(solution)/shard_map/jit(_take)/gather | solution.py:21
  45.9 20.0 %gather.7 = bf16[7680,512]{1,0:T(8,128)(2,1)} reshape(bf16[2560,3,512]{2,1,0:T(4,128)(2,1)} %gather_fusion) | data formatting | bytes 15728640 | tf_op jit(solution)/shard_map/jit(_take)/gather | solution.py:21
  65.9 1.3 broadcast_in_dim.18
  67.2 1.1 broadcast_in_dim.19
  68.3 16.5 %fusion.4 = f32[1024,512]{0,1:T(8,128)} fusion(bf16[1024,7680]{1,0:T(8,128)(2,1)} %param.4, bf16[7680,512]{1,0:T(8,128)(2,1)} %gather.7, pred[7680]{0:T(1024)(128)(4,1)S(1)} %broadcast_in_dim.19), kind=kOutput, calls=%fused_computation.15 | convolution fusion | flops 8056995840 | bytes 25697792 | tf_op jit(solution)/shard_map/dot_general | solution.py:44
  84.8 0.0 all-reduce.5.cloned.1.call-update
  84.9 0.0 all-reduce.7.cloned.1.call-start
  84.9 72.3 %all-reduce.5.cloned.1.call-done = f32[1024,512]{0,1:T(8,128)} async-done(((f32[1024,512]{0,1:T(8,128)}), f32[1024,512]{0,1:T(8,128)}) %all-reduce.5.cloned.1.call-update) | async-done | bytes 2097168 | tf_op jit(solution)/shard_map/psum | solution.py:45
  157.2 0.0 copy-start
  157.2 1.9 multiply_reduce_fusion
  159.1 16.4 %psum.29 = f32[1024]{0:T(1024)S(1)} all-reduce(f32[1024]{0:T(1024)S(1)} %multiply_reduce_fusion), channel_id=1, replica_groups=mesh['row'=4,'col'=8] {'col'}, use_global_device_ids=true, to_apply=%region_2.3 | all-reduce | flops 1024 | bytes 8192 | tf_op jit(solution)/shard_map/psum | solution.py:46
  175.5 0.0 copy-done
  175.5 1.4 broadcast_select_fusion
  176.9 0.0 copy-start.2
  176.9 1.1 broadcast_select_fusion.1
  178.0 0.0 all-reduce.7.cloned.1.call-update
  178.0 0.0 copy-done.2
  178.0 0.7 fusion.24
  198.4 42.2 %all-reduce.7.cloned.1.call-done = (bf16[1024,512]{0,1:T(8,128)(2,1)}, bf16[1024,512]{0,1:T(8,128)(2,1)}) async-done(((bf16[1024,512]{0,1:T(8,128)(2,1)}, bf16[1024,512]{0,1:T(8,128)(2,1)}), (bf16[1024,512]{0,1:T(8,128)(2,1)}, bf16[1024,512]{0,1:T(8,128)(2,1)})) %all-reduce.7.cloned.1.call-update) | async-done | bytes 2097168 | tf_op jit(solution)/shard_map/psum | solution.py:16
  240.6 0.0 copy-start.1
  240.6 1.4 constant_dynamic-update-slice_fusion.1
  242.0 0.2 copy-done.1
  242.2 0.1 constant_dynamic-update-slice_fusion
  242.2 1.4 bitcast_dynamic-update-slice_fusion.7
  243.6 1.4 bitcast_dynamic-update-slice_fusion.6
  245.0 1.4 bitcast_dynamic-update-slice_fusion.5
  246.4 1.4 bitcast_dynamic-update-slice_fusion.4
  247.8 1.4 bitcast_dynamic-update-slice_fusion.3
  249.1 1.4 bitcast_dynamic-update-slice_fusion.2
  250.5 1.4 bitcast_dynamic-update-slice_fusion.1
  251.9 0.0 copy-start.3
  251.9 6.2 %copy-done.3 = f32[8,1024,512]{2,1,0:T(8,128)} copy-done((f32[8,1024,512]{2,1,0:T(8,128)}, f32[8,1024,512]{2,1,0:T(8,128)S(1)}, u32[]{:S(2)}) %copy-start.3) | copy-done | bytes 16777240
  258.1 2.7 %bitcast_dynamic-update-slice_fusion = f32[8,1024,512]{2,1,0:T(8,128)} fusion(f32[8,1024,512]{2,1,0:T(8,128)} %copy-done.3, bf16[1024,1024]{0,1:T(8,128)(2,1)S(1)} %constant_dynamic-update-slice_fusion, s32[]{:T(128)S(6)} %select_n.61, bf16[1024,512]{0,1:T(8,128)(2,1)S(1)} %get-tuple-element.8, f32[]{:T(128)S(6)} %rsqrt.35), kind=kOutput, calls=%fused_computation.5 | convolution fusion | flops 1074266112 | bytes 5242888 | tf_op jit(solution)/shard_map/dot_general | solution.py:33
  (2 shorter events, 0.0 us)
Async XLA Ops:
  6.5 150.7 %all-reduce.5.cloned.1.call-start = ((), (), s32[]{:S(2)}) async-start(), calls=%async_computation | async-start | bytes 4194304 | tf_op jit(solution)/shard_map/psum | solution.py:45
  84.9 155.8 %all-reduce.7.cloned.1.call-start = ((), (), s32[]{:S(2)}) async-start(), calls=%async_computation.1 | async-start | bytes 4194304 | tf_op jit(solution)/shard_map/psum | solution.py:16
  157.2 18.3 %copy-start = (f32[1024,512]{0,1:T(8,128)S(1)}, f32[1024,512]{0,1:T(8,128)}, u32[]{:S(2)}) copy-start(f32[1024,512]{0,1:T(8,128)} %all-reduce.5.cloned.1.call-done) | copy-start | bytes 6291460
  176.9 1.1 copy-start.2
  240.6 1.5 copy-start.1
  251.9 6.2 %copy-start.3 = (f32[8,1024,512]{2,1,0:T(8,128)}, f32[8,1024,512]{2,1,0:T(8,128)S(1)}, u32[]{:S(2)}) copy-start(f32[8,1024,512]{2,1,0:T(8,128)S(1)} %bitcast_dynamic-update-slice_fusion.1) | copy-start | bytes 50331652
Sparse Core Ops, SparseCore 0:
  85.0 72.1 all-reduce.4
  178.1 62.4 all-reduce.6
where the time goes:
time: 269 us; the launch traced here: 268 us
  waiting for transfers between devices  115 us (43%)
  local copies, waits for them, and re-layouts  68.8 us (26%)
  between operations  33.2 us (12%)
  matrix products  28.8 us (11%)
  blocking collectives  16.4 us (6%)
  other arithmetic  5.85 us (2%)
    psum x1, waiting for transfers between devices, local(): projected = lax.psum(partial_terms, 'row')  72.3 us
    psum x1, waiting for transfers between devices, from_root(): return lax.psum(block, axis)  42.2 us
    gather x2, local copies, waits for them, and re-layouts, reorder(): return jnp.take(per_atom, atom_slot, axis=0).reshape(modes_panel.shape)  37.2 us
    reshape x1, local copies, waits for them, and re-layouts, reorder(): per_atom = modes_panel.reshape(atom_slot.shape[0], 3, modes_panel.shape[1])  20.7 us
    dot_general x1, matrix products, local(): jnp.dot(velocities, panel, preferred_element_type=jnp.float32)  16.5 us
    psum x1, blocking collectives, local(): energy = lax.psum(jnp.sum(projected * projected, axis=1), 'col')  16.4 us
    dot_general x8, matrix products, correlate(): lax.dot_general(row_modes, shifted, (((0,), (0,)), ((), ())), preferred_e...  12.3 us
    unnamed x9, local copies, waits for them, and re-layouts  7.7 us
  transfers between devices with their start and end apart: 2, of which 2 were waited for; matrix products, arithmetic and copies ran while one was open for 0% of the time, Pallas kernels for 0%

commit v1 on v0

v1 whole, which is shorter than its diff:
```python
import functools

import jax
import jax.numpy as jnp
from jax import lax
from jax.experimental import pallas as pl
from jax.experimental.pallas import tpu as pltpu
from jax.sharding import PartitionSpec as P

MAXLAG = 256
LANES = 128
ROWS = 8
GROUP = 16

epsilon = 1e-06


def swap(block, axis, offset):
    size = lax.axis_size(axis)
    return lax.ppermute(block, axis, [(i, i ^ offset) for i in range(size)])


def reorder_kernel(slot, panel, out, staged, source, in_sems, ordered, out_sem, *, chunk):
    depth, width = panel.shape
    blocks = width // LANES
    copies = [
        pltpu.make_async_copy(
            panel.at[pl.ds(c * chunk, chunk), :], staged.at[pl.ds(c * chunk, chunk), :], in_sems.at[c]
        )
        for c in range(depth // chunk)
    ]
    for copy in copies:
        copy.start()
    for c, copy in enumerate(copies):
        copy.wait()

        def widen(i, carry):
            first = pl.multiple_of(c * chunk + i * 64, 64)
            for j in range(blocks):
                source[j, pl.ds(ROWS + first, 64), :] = staged[
                    pl.ds(first, 64), j * LANES : (j + 1) * LANES
                ].astype(jnp.float32)
            return carry

        lax.fori_loop(0, chunk // 64, widen, 0)
    row = lax.broadcasted_iota(jnp.int32, (ROWS, LANES), 0)

    def move(g, carry):
        base = [slot[g * GROUP + i] * 3 for i in range(GROUP)]
        for j in range(blocks):
            tiles = []
            for v in range(3 * GROUP // ROWS):
                tile = None
                for i in range(GROUP):
                    low = 3 * i - ROWS * v
                    if low + 3 <= 0 or low >= ROWS:
                        continue
                    piece = source[j, pl.ds(base[i] + (ROWS - low), ROWS), :]
                    tile = piece if tile is None else jnp.where(row >= low, piece, tile)
                tiles.append(tile)
            ordered[
                pl.ds(pl.multiple_of(g * 3 * GROUP, GROUP), 3 * GROUP), j * LANES : (j + 1) * LANES
            ] = jnp.concatenate(tiles, axis=0).astype(jnp.bfloat16)
        return carry

    lax.fori_loop(0, slot.shape[0] // GROUP, move, 0)
    copy = pltpu.make_async_copy(ordered, out, out_sem)
    copy.start()
    copy.wait()


def reorder(panel, slot):
    depth, width = panel.shape
    chunk = depth // 10
    return pl.pallas_call(
        functools.partial(reorder_kernel, chunk=chunk),
        out_shape=jax.ShapeDtypeStruct((depth, width), jnp.bfloat16),
        grid_spec=pltpu.PrefetchScalarGridSpec(
            num_scalar_prefetch=1,
            grid=(1,),
            in_specs=[pl.BlockSpec(memory_space=pl.ANY)],
            out_specs=pl.BlockSpec(memory_space=pl.ANY),
            scratch_shapes=[
                pltpu.VMEM((depth, width), jnp.bfloat16),
                pltpu.VMEM((width // LANES, depth + 2 * ROWS, LANES), jnp.float32),
                pltpu.SemaphoreType.DMA((depth // chunk,)),
                pltpu.VMEM((depth, width), jnp.bfloat16),
                pltpu.SemaphoreType.DMA,
            ],
        ),
        cost_estimate=pl.CostEstimate(flops=0, bytes_accessed=4 * depth * width, transcendentals=0),
        name="reorder",
    )(slot, panel)


def shift_kernel(scalars, *refs, parts, lags):
    pieces, out, source = refs[:parts], refs[parts], refs[parts + 1]
    blocks, length, _ = source.shape
    size = pieces[0].shape[0]
    snapshots = parts * size

    @pl.when(pl.program_id(0) == 0)
    def _():
        for j in range(blocks):
            columns = slice(j * LANES, (j + 1) * LANES)
            for m, piece in enumerate(pieces):
                start = pl.multiple_of((scalars[lags] ^ m) * size, size)
                source[j, pl.ds(start, size), :] = piece[:, columns].astype(jnp.float32)
            source[j, snapshots:, :] = jnp.zeros((length - snapshots, LANES), jnp.float32)

    offset = scalars[pl.program_id(0)]
    step = 128

    def body(i, carry):
        first = pl.multiple_of(i * step, step)
        for j in range(blocks):
            out[0, pl.ds(first, step), j * LANES : (j + 1) * LANES] = source[
                j, pl.ds(first + offset, step), :
            ].astype(jnp.bfloat16)
        return carry

    lax.fori_loop(0, snapshots // step, body, 0)


def shifted_copies(pieces, lag_offsets, mine):
    size, width = pieces[0].shape
    parts = len(pieces)
    snapshots = size * parts
    lags = lag_offsets.shape[0]
    scalars = jnp.concatenate([lag_offsets, mine.astype(jnp.int32)[None]])
    whole = pl.BlockSpec((size, width), lambda l, s: (0, 0))
    return pl.pallas_call(
        functools.partial(shift_kernel, parts=parts, lags=lags),
        out_shape=jax.ShapeDtypeStruct((lags, snapshots, width), jnp.bfloat16),
        grid_spec=pltpu.PrefetchScalarGridSpec(
            num_scalar_prefetch=1,
            grid=(lags,),
            in_specs=[whole] * parts,
            out_specs=pl.BlockSpec((1, snapshots, width), lambda l, s: (l, 0, 0)),
            scratch_shapes=[pltpu.VMEM((width // LANES, snapshots + MAXLAG + ROWS, LANES), jnp.float32)],
        ),
        cost_estimate=pl.CostEstimate(
            flops=0, bytes_accessed=2 * snapshots * width * (lags + 1), transcendentals=0
        ),
        name="shift",
    )(scalars, *pieces)


def correlate_kernel(scalars, factors, *refs, parts, size):
    pieces, shifted, out, turned = refs[:parts], refs[parts], refs[-2], refs[-1]

    @pl.when(pl.program_id(0) == 0)
    def _():
        for m, piece in enumerate(pieces):
            start = pl.multiple_of((scalars[0] ^ m) * size, size)
            turned[:, pl.ds(start, size)] = piece[...].T

    product = jnp.dot(turned[...], shifted[0], preferred_element_type=jnp.float32)
    out[0] = product * factors[pl.program_id(0)]


def correlate(pieces, shifted, factors, mine, owner, out_shape, previous):
    size, modes = pieces[0].shape
    parts = len(pieces)
    lags, snapshots, width = shifted.shape
    scalars = jnp.stack([mine, owner]).astype(jnp.int32)
    in_specs = [pl.BlockSpec((size, modes), lambda l, s, f: (0, 0))] * parts
    in_specs.append(pl.BlockSpec((1, snapshots, width), lambda l, s, f: (l, 0, 0)))
    operands = [*pieces, shifted]
    aliases = {}
    if previous is not None:
        aliases = {len(operands) + 2: 0}
        operands.append(previous)
        in_specs.append(pl.BlockSpec(memory_space=pl.ANY))
    return pl.pallas_call(
        functools.partial(correlate_kernel, parts=parts, size=size),
        out_shape=jax.ShapeDtypeStruct(out_shape, jnp.float32),
        grid_spec=pltpu.PrefetchScalarGridSpec(
            num_scalar_prefetch=2,
            grid=(lags,),
            in_specs=in_specs,
            out_specs=pl.BlockSpec((1, modes, width), lambda l, s, f: (l, s[1], 0)),
            scratch_shapes=[pltpu.VMEM((modes, snapshots), jnp.bfloat16)],
        ),
        input_output_aliases=aliases,
        cost_estimate=pl.CostEstimate(
            flops=2 * lags * modes * snapshots * width,
            bytes_accessed=lags * width * (2 * snapshots + 4 * modes),
            transcendentals=0,
        ),
        name="correlate",
    )(scalars, factors, *operands)


def reduce_scatter(pieces):
    ranks = len(pieces)
    bits = [1 << b for b in range(ranks.bit_length() - 1)]
    width = pieces[0].shape[1]
    halves = []
    for half, order in enumerate((bits, bits[::-1])):
        columns = slice(half * width // 2, (half + 1) * width // 2)
        held = [piece[:, columns] for piece in pieces]
        live = range(ranks)
        for bit in order:
            for m in reversed(live):
                if m & bit:
                    held[m ^ bit] = held[m ^ bit] + swap(held[m], "row", bit)
            live = [m for m in live if not m & bit]
        halves.append(held[0])
    return halves


def local(velocities, modes_panel, atom_slot, lag_offsets):
    ranks = lax.axis_size("row")
    columns = lax.axis_size("col")
    owners = columns // ranks
    mine = lax.axis_index("row")
    group = lax.axis_index("col") // owners
    member = lax.axis_index("col") % owners
    snapshots = velocities.shape[0]
    size = snapshots // ranks
    width = modes_panel.shape[1]
    modes = width * columns

    panel = reorder(modes_panel, atom_slot)
    pieces = [None] * ranks
    for m in reversed(range(ranks)):
        rows = lax.dynamic_slice_in_dim(velocities, (mine ^ m) * size, size, 0)
        pieces[m] = jnp.dot(rows, panel, preferred_element_type=jnp.float32)
    halves = reduce_scatter(pieces)

    energy = sum(jnp.sum(half * half, axis=1) for half in halves)
    bit = 1
    while bit < columns:
        energy = energy + swap(energy, "col", bit)
        bit *= 2
    scale = lax.rsqrt(energy / modes + epsilon)[:, None]
    own = jnp.concatenate([(half * scale).astype(jnp.bfloat16) for half in halves], axis=1)

    across = [own] + [swap(own, "col", owners * m) for m in range(1, ranks)]
    column_pieces = [own] + [swap(own, "row", m) for m in range(1, ranks)]
    shifted = shifted_copies(column_pieces, lag_offsets, mine)

    stacked = jnp.stack(across)
    row_pieces = []
    for m in range(ranks):
        chosen = lax.dynamic_index_in_dim(stacked, group ^ mine ^ m, 0, keepdims=False)
        row_pieces.append(chosen if m == 0 else swap(chosen, "row", m))

    factors = lax.rsqrt((snapshots - lag_offsets).astype(jnp.float32))
    out_shape = (lag_offsets.shape[0], width * owners, width)
    others = [[swap(piece, "col", k) for piece in row_pieces] for k in range(1, owners)]
    result = correlate(row_pieces, shifted, factors, mine, member, out_shape, None)
    for k in range(1, owners):
        result = correlate(others[k - 1], shifted, factors, mine, member ^ k, out_shape, result)
    return result


def solution(mesh):
    return jax.shard_map(
        local,
        mesh=mesh,
        in_specs=(P(None, "row"), P("row", "col"), P("row"), P()),
        out_specs=P(None, "row", "col"),
        check_vma=False,
    )
```

time: 269 us -> 125 us (0.46)
  waiting for transfers between devices: 115 us -> 25.4 us
  local copies, waits for them, and re-layouts: 68.8 us -> 3.08 us
  Pallas kernels: 0 us -> 43.3 us
  between operations: 33.2 us -> 0.28 us
  starting transfers between devices: 0.04 us -> 24.1 us
  blocking collectives: 16.4 us -> 0 us
  other arithmetic: 5.85 us -> 2.29 us
    psum x2 -> x0, waiting for transfers between devices: 114 us -> none  [the longest x1 72.3 us: local(): projected = lax.psum(partial_terms, 'row')]
    pallas_call x0 -> x4, Pallas kernels: none -> 43.3 us  [the longest x2 24.3 us: correlate(): pl.pallas_call(functools.partial(correlate_kernel, parts=parts, size=size...]
    gather x2 -> x0, local copies, waits for them, and re-layouts: 37.2 us -> none  [reorder(): return jnp.take(per_atom, atom_slot, axis=0).reshape(modes_panel.shape)]
    ppermute x0 -> x22, waiting for transfers between devices: none -> 25.4 us  [swap(): return lax.ppermute(block, axis, [(i, i ^ offset) for i in range(size)])]
    ppermute x0 -> x22, starting transfers between devices: none -> 24.1 us  [swap(): return lax.ppermute(block, axis, [(i, i ^ offset) for i in range(size)])]
    reshape x1 -> x0, local copies, waits for them, and re-layouts: 20.7 us -> none  [reorder(): per_atom = modes_panel.reshape(atom_slot.shape[0], 3, modes_panel.shape[1])]
    psum x1 -> x0, blocking collectives: 16.4 us -> none  [local(): energy = lax.psum(jnp.sum(projected * projected, axis=1), 'col')]
    unnamed x9 -> x26, local copies, waits for them, and re-layouts: 7.7 us -> 2.96 us
  transfers between devices with their start and end apart: 2 -> 22, of which waited for: 2 -> 7; matrix products, arithmetic and copies ran while one was open for 0% -> 18% of each run, Pallas kernels for 0% -> 15%
where the time goes in v1:
time: 125 us
  Pallas kernels  43.3 us (35%)
  matrix products  26.5 us (21%)
  waiting for transfers between devices  25.4 us (20%)
  starting transfers between devices  24.1 us (19%)
  local copies, waits for them, and re-layouts  3.08 us (2%)
  other arithmetic  2.29 us (2%)
    dot_general x4, matrix products, local(): pieces[m] = jnp.dot(rows, panel, preferred_element_type=jnp.float32)  26.5 us
    ppermute x22, waiting for transfers between devices, swap(): return lax.ppermute(block, axis, [(i, i ^ offset) for i in range(size)])  25.4 us
    pallas_call x2, Pallas kernels, correlate(): pl.pallas_call(functools.partial(correlate_kernel, parts=parts, size=size...  24.3 us
    ppermute x22, starting transfers between devices, swap(): return lax.ppermute(block, axis, [(i, i ^ offset) for i in range(size)])  24.1 us
    pallas_call x1, Pallas kernels, reorder(): pl.pallas_call(functools.partial(reorder_kernel, chunk=chunk), out_shape=...  11.8 us
    pallas_call x1, Pallas kernels, shifted_copies(): pl.pallas_call(functools.partial(shift_kernel, parts=parts, lags=lags), o...  7.2 us
    unnamed x26, local copies, waits for them, and re-layouts  2.96 us
  transfers between devices with their start and end apart: 22, of which 7 were waited for; matrix products, arithmetic and copies ran while one was open for 18% of the time, Pallas kernels for 15%

profile of v1, /device:TPU:0, one launch (start us, length us, event | category | flops | bytes accessed | tf_op | source)
XLA Modules:
  0.0 124.9 jit_solution(12473996043222783961)
XLA Ops:
  0.0 11.8 %reorder.1 = bf16[7680,512]{1,0:T(8,128)(2,1)} custom-call(s32[2560]{0:T(1024)} %slot.1, bf16[7680,512]{1,0:T(8,128)(2,1)} %panel.1), custom_call_target="tpu_custom_call" | custom-call | bytes 15728640 | tf_op jit(solution)/shard_map/reorder/pallas_call | solution.py:75
  11.8 6.6 %fusion = f32[256,512]{1,0:T(8,128)S(1)} fusion(bf16[7680,512]{1,0:T(8,128)(2,1)} %reorder.1, bf16[1024,7680]{1,0:T(8,128)(2,1)} %param.4, s32[]{:T(128)S(6)} %select_n.40), kind=kOutput, calls=%fused_computation | convolution fusion | flops 2013265920 | bytes 12320772 | tf_op jit(solution)/shard_map/dot_general | solution.py:229
  18.5 3.0 %collective-permute-start.1 = (f32[256,256]{1,0:T(8,128)S(1)}, f32[256,256]{1,0:T(8,128)S(1)}, u32[]{:S(2)}, u32[]{:S(2)}) collective-permute-start(f32[256,256]{1,0:T(8,128)S(1)} %get-tuple-element.17), channel_id=1, source_target_pairs={{0,8},{8,0},{16,24},{24,16},{1,9},{9,1},{17,25},{25,17},{2,10},{10... | collective-permute-start | bytes 786440 | tf_op jit(solution)/shard_map/ppermute | solution.py:20
  21.5 1.6 %collective-permute-start.4 = (f32[256,256]{1,0:T(8,128)S(1)}, f32[256,256]{1,0:T(8,128)S(1)}, u32[]{:S(2)}, u32[]{:S(2)}) collective-permute-start(f32[256,256]{1,0:T(8,128)S(1)} %get-tuple-element.18), channel_id=1, source_target_pairs={{0,16},{8,24},{16,0},{24,8},{1,17},{9,25},{17,1},{25,9},{2,18},{10... | collective-permute-start | bytes 786440 | tf_op jit(solution)/shard_map/ppermute | solution.py:20
  23.1 6.6 %fusion.2 = f32[256,512]{1,0:T(8,128)S(1)} fusion(bf16[7680,512]{1,0:T(8,128)(2,1)} %reorder.1, bf16[1024,7680]{1,0:T(8,128)(2,1)} %param.4, s32[]{:T(128)S(6)} %select_n.39), kind=kOutput, calls=%fused_computation.2 | convolution fusion | flops 2013265920 | bytes 12320772 | tf_op jit(solution)/shard_map/dot_general | solution.py:229
  29.7 6.6 %fusion.4 = f32[256,512]{1,0:T(8,128)S(1)} fusion(bf16[7680,512]{1,0:T(8,128)(2,1)} %reorder.1, bf16[1024,7680]{1,0:T(8,128)(2,1)} %param.4, s32[]{:T(128)S(6)} %select_n.38), kind=kOutput, calls=%fused_computation.4 | convolution fusion | flops 2013265920 | bytes 12320772 | tf_op jit(solution)/shard_map/dot_general | solution.py:229
  36.3 0.1 fusion.15
  36.4 0.6 collective-permute-start
  37.0 1.5 %collective-permute-start.5 = (f32[256,256]{1,0:T(8,128)S(1)}, f32[256,256]{1,0:T(8,128)S(1)}, u32[]{:S(2)}, u32[]{:S(2)}) collective-permute-start(f32[256,256]{1,0:T(8,128)S(1)} %get-tuple-element.14), channel_id=1, source_target_pairs={{0,8},{8,0},{16,24},{24,16},{1,9},{9,1},{17,25},{25,17},{2,10},{10... | collective-permute-start | bytes 786440 | tf_op jit(solution)/shard_map/ppermute | solution.py:20
  38.5 0.5 collective-permute-start.2
  39.0 1.6 %collective-permute-start.3 = (f32[256,256]{1,0:T(8,128)S(1)}, f32[256,256]{1,0:T(8,128)S(1)}, u32[]{:S(2)}, u32[]{:S(2)}) collective-permute-start(f32[256,256]{1,0:T(8,128)S(1)} %get-tuple-element.16), channel_id=1, source_target_pairs={{0,16},{8,24},{16,0},{24,8},{1,17},{9,25},{17,1},{25,9},{2,18},{10... | collective-permute-start | bytes 786440 | tf_op jit(solution)/shard_map/ppermute | solution.py:20
  40.6 6.6 %fusion.6 = f32[256,512]{1,0:T(8,128)S(1)} fusion(bf16[7680,512]{1,0:T(8,128)(2,1)} %reorder.1, bf16[1024,7680]{1,0:T(8,128)(2,1)} %param.4, s32[]{:T(128)S(6)} %select_n.37), kind=kOutput, calls=%fused_computation.6 | convolution fusion | flops 2013265920 | bytes 12320772 | tf_op jit(solution)/shard_map/dot_general | solution.py:229
  47.2 0.0 copy-start.12
  47.2 0.0 collective-permute-done
  47.3 2.3 %collective-permute-done.5 = f32[256,256]{1,0:T(8,128)S(1)} collective-permute-done((f32[256,256]{1,0:T(8,128)S(1)}, f32[256,256]{1,0:T(8,128)S(1)}, u32[]{:S(2)}, u32[]{:S(2)}) %collective-permute-start.5) | collective-permute-done | bytes 262176 | tf_op jit(solution)/shard_map/ppermute | solution.py:20
  49.5 0.0 collective-permute-done.2
  49.5 1.6 %collective-permute-done.3 = f32[256,256]{1,0:T(8,128)S(1)} collective-permute-done((f32[256,256]{1,0:T(8,128)S(1)}, f32[256,256]{1,0:T(8,128)S(1)}, u32[]{:S(2)}, u32[]{:S(2)}) %collective-permute-start.3) | collective-permute-done | bytes 262176 | tf_op jit(solution)/shard_map/ppermute | solution.py:20
  51.1 0.2 multiply_reduce_fusion
  51.3 0.1 collective-permute-start.6
  51.4 1.1 collective-permute-done.6
  52.5 1.6 %collective-permute-start.7 = (f32[256]{0:T(256)S(1)}, f32[256]{0:T(256)S(1)}, u32[]{:S(2)}, u32[]{:S(2)}) collective-permute-start(f32[256]{0:T(256)S(1)} %add.78), channel_id=1, source_target_pairs={{0,2},{1,3},{2,0},{3,1},{4,6},{5,7},{6,4},{7,5},{8,10},{9,11},{10,... | collective-permute-start | bytes 3080 | tf_op jit(solution)/shard_map/ppermute | solution.py:20
  54.1 2.0 %collective-permute-done.7 = f32[256]{0:T(256)S(1)} collective-permute-done((f32[256]{0:T(256)S(1)}, f32[256]{0:T(256)S(1)}, u32[]{:S(2)}, u32[]{:S(2)}) %collective-permute-start.7) | collective-permute-done | bytes 1056 | tf_op jit(solution)/shard_map/ppermute | solution.py:20
  56.1 2.6 %collective-permute-start.8 = (f32[256]{0:T(256)S(1)}, f32[256]{0:T(256)S(1)}, u32[]{:S(2)}, u32[]{:S(2)}) collective-permute-start(f32[256]{0:T(256)S(1)} %add.79), channel_id=1, source_target_pairs={{0,4},{1,5},{2,6},{3,7},{4,0},{5,1},{6,2},{7,3},{8,12},{9,13},{10,... | collective-permute-start | bytes 3080 | tf_op jit(solution)/shard_map/ppermute | solution.py:20
  58.7 1.9 %collective-permute-done.8 = f32[256]{0:T(256)S(1)} collective-permute-done((f32[256]{0:T(256)S(1)}, f32[256]{0:T(256)S(1)}, u32[]{:S(2)}, u32[]{:S(2)}) %collective-permute-start.8) | collective-permute-done | bytes 1056 | tf_op jit(solution)/shard_map/ppermute | solution.py:20
  60.6 0.1 multiply_convert_fusion.1
  60.8 0.0 copy-start.1
  60.8 3.7 %collective-permute-start.11 = (bf16[256,512]{1,0:T(8,128)(2,1)S(1)}, bf16[256,512]{1,0:T(8,128)(2,1)S(1)}, u32[]{:S(2)}, u32[]{:S(2)}) collective-permute-start(bf16[256,512]{1,0:T(8,128)(2,1)S(1)} %get-tuple-element.20.refs_0_), channel_id=1, source_target_pairs={{0,6},{1,7},{2,4},{3,5},{4,2},{5,3},{6,0},{7,1},{8,14},{9,15},{10,... | collective-permute-start | bytes 786440 | tf_op jit(solution)/shard_map/ppermute | solution.py:20
  64.4 0.0 collective-permute-start.10
  64.4 0.8 collective-permute-start.9
  65.2 0.6 pad_add_fusion
  65.8 0.3 collective-permute-start.21
  66.1 1.7 %collective-permute-start.20 = (bf16[256,512]{1,0:T(8,128)(2,1)S(1)}, bf16[256,512]{1,0:T(8,128)(2,1)S(1)}, u32[]{:S(2)}, u32[]{:S(2)}) collective-permute-start(bf16[256,512]{1,0:T(8,128)(2,1)S(1)} %get-tuple-element.20.refs_0_), channel_id=1, source_target_pairs={{0,16},{8,24},{16,0},{24,8},{1,17},{9,25},{17,1},{25,9},{2,18},{10... | collective-permute-start | bytes 786440 | tf_op jit(solution)/shard_map/ppermute | solution.py:20
  67.8 4.0 %collective-permute-done.11 = bf16[256,512]{1,0:T(8,128)(2,1)S(1)} collective-permute-done((bf16[256,512]{1,0:T(8,128)(2,1)S(1)}, bf16[256,512]{1,0:T(8,128)(2,1)S(1)}, u32[]{:S(2)}, u32[]{:S(2)}) %collective-permute-start.11) | collective-permute-done | bytes 262176 | tf_op jit(solution)/shard_map/ppermute | solution.py:20
  71.8 0.5 collective-permute-start.19
  72.3 12.4 %collective-permute-done.10 = bf16[256,512]{1,0:T(8,128)(2,1)S(1)} collective-permute-done((bf16[256,512]{1,0:T(8,128)(2,1)S(1)}, bf16[256,512]{1,0:T(8,128)(2,1)S(1)}, u32[]{:S(2)}, u32[]{:S(2)}) %collective-permute-start.10) | collective-permute-done | bytes 262176 | tf_op jit(solution)/shard_map/ppermute | solution.py:20
  84.8 0.0 collective-permute-done.9
  84.8 0.1 pad_maximum_fusion
  84.9 0.1 dynamic-slice_bitcast_fusion
  85.0 0.5 collective-permute-start.17
  85.5 1.5 %collective-permute-start.15 = (bf16[256,512]{1,0:T(8,128)(2,1)S(1)}, bf16[256,512]{1,0:T(8,128)(2,1)S(1)}, u32[]{:S(2)}, u32[]{:S(2)}) collective-permute-start(bf16[256,512]{1,0:T(8,128)(2,1)S(1)} %get-tuple-element.8), channel_id=1, source_target_pairs={{0,16},{8,24},{16,0},{24,8},{1,17},{9,25},{17,1},{25,9},{2,18},{10... | collective-permute-start | bytes 786440 | tf_op jit(solution)/shard_map/ppermute | solution.py:20
  87.1 0.0 collective-permute-done.21.refs_3_
  87.1 1.5 %collective-permute-start.13 = (bf16[256,512]{1,0:T(8,128)(2,1)S(1)}, bf16[256,512]{1,0:T(8,128)(2,1)S(1)}, u32[]{:S(2)}, u32[]{:S(2)}) collective-permute-start(bf16[256,512]{1,0:T(8,128)(2,1)S(1)} %get-tuple-element.9), channel_id=1, source_target_pairs={{0,8},{8,0},{16,24},{24,16},{1,9},{9,1},{17,25},{25,17},{2,10},{10... | collective-permute-start | bytes 786440 | tf_op jit(solution)/shard_map/ppermute | solution.py:20
  88.6 0.6 pad_add_fusion.1.scalars
  89.2 0.5 convert_rsqrt_fusion.factors
  89.7 0.0 collective-permute-done.20.refs_2_
  89.7 0.0 collective-permute-start.12
  89.8 0.7 copy-done.10
  90.4 0.7 copy-done.11
  91.1 7.2 %shift.1.refs_4_ = bf16[8,1024,512]{2,1,0:T(8,128)(2,1)} custom-call(s32[9]{0:T(128)} %pad_add_fusion.1.scalars, bf16[256,512]{1,0:T(8,128)(2,1)} %copy-done.1, bf16[256,512]{1,0:T(8,128)(2,1)} %copy-done.11, bf16[256,512]{1,0:T(8,128)(2,1)} %copy-done.10, bf16[256,512]{1,0:T(8,128)(2,1)} %copy-done.9), custom_call_target="tpu_custom_call" | custom-call | bytes 9437184 | tf_op jit(solution)/shard_map/shift/pallas_call | solution.py:132
  98.3 0.0 collective-permute-start.18
  98.3 0.0 collective-permute-done.15.refs_2_
  98.3 0.5 collective-permute-start.16
  98.8 0.0 collective-permute-done.13.refs_1_
  98.8 0.1 collective-permute-start.14
  98.9 0.1 copy-done.2
  99.0 0.1 copy-done.3
  99.1 0.5 copy-done.4
  99.6 12.1 %correlate.2.refs_5_ = f32[8,1024,512]{2,1,0:T(8,128)} custom-call(s32[2]{0:T(128)} %get-tuple-element.22.scalars, f32[8]{0:T(128)} %convert_rsqrt_fusion.factors, bf16[256,512]{1,0:T(8,128)(2,1)} %copy-done, bf16[256,512]{1,0:T(8,128)(2,1)} %copy-done.4, bf16[256,512]{1,0:T(8,128)(2,1)} %copy-done.3, bf16[256,512]{1,0:T(8,128)(2,1)} %copy-done.2, ...), custom_call_target="tpu_custom_call" | custom-call | flops 4294967296 | bytes 16777216 | tf_op jit(solution)/shard_map/correlate/pallas_call | solution.py:175
  111.7 0.0 collective-permute-done.12.refs_0_
  111.8 0.7 copy-done.5
  112.4 0.1 copy-done.6
  112.5 0.1 copy-done.7
  112.6 0.1 copy-done.8
  112.7 12.1 %correlate.3 = f32[8,1024,512]{2,1,0:T(8,128)} custom-call(s32[2]{0:T(128)} %get-tuple-element.21.scalars, f32[8]{0:T(128)} %convert_rsqrt_fusion.factors, bf16[256,512]{1,0:T(8,128)(2,1)} %copy-done.5, bf16[256,512]{1,0:T(8,128)(2,1)} %copy-done.8, bf16[256,512]{1,0:T(8,128)(2,1)} %copy-done.7, ...), custom_call_target="tpu_custom_call", output_to_operand_aliasing={{}: (7, {})} | custom-call | flops 4294967296 | bytes 16777216 | tf_op jit(solution)/shard_map/correlate/pallas_call | solution.py:175
  (29 shorter events, 0.2 us)
Async XLA Ops:
  18.5 20.0 %collective-permute-start.1 = (f32[256,256]{1,0:T(8,128)S(1)}, f32[256,256]{1,0:T(8,128)S(1)}, u32[]{:S(2)}, u32[]{:S(2)}) collective-permute-start(f32[256,256]{1,0:T(8,128)S(1)} %get-tuple-element.17), channel_id=1, source_target_pairs={{0,8},{8,0},{16,24},{24,16},{1,9},{9,1},{17,25},{25,17},{2,10},{10... | collective-permute-start | bytes 786440 | tf_op jit(solution)/shard_map/ppermute | solution.py:20
  21.5 14.8 %collective-permute-start.4 = (f32[256,256]{1,0:T(8,128)S(1)}, f32[256,256]{1,0:T(8,128)S(1)}, u32[]{:S(2)}, u32[]{:S(2)}) collective-permute-start(f32[256,256]{1,0:T(8,128)S(1)} %get-tuple-element.18), channel_id=1, source_target_pairs={{0,16},{8,24},{16,0},{24,8},{1,17},{9,25},{17,1},{25,9},{2,18},{10... | collective-permute-start | bytes 786440 | tf_op jit(solution)/shard_map/ppermute | solution.py:20
  36.4 10.9 %collective-permute-start = (f32[256,256]{1,0:T(8,128)S(1)}, f32[256,256]{1,0:T(8,128)S(1)}, u32[]{:S(2)}, u32[]{:S(2)}) collective-permute-start(f32[256,256]{1,0:T(8,128)S(1)} %get-tuple-element.13), channel_id=1, source_target_pairs={{0,8},{8,0},{16,24},{24,16},{1,9},{9,1},{17,25},{25,17},{2,10},{10... | collective-permute-start | bytes 786440 | tf_op jit(solution)/shard_map/ppermute | solution.py:20
  37.0 12.6 %collective-permute-start.5 = (f32[256,256]{1,0:T(8,128)S(1)}, f32[256,256]{1,0:T(8,128)S(1)}, u32[]{:S(2)}, u32[]{:S(2)}) collective-permute-start(f32[256,256]{1,0:T(8,128)S(1)} %get-tuple-element.14), channel_id=1, source_target_pairs={{0,8},{8,0},{16,24},{24,16},{1,9},{9,1},{17,25},{25,17},{2,10},{10... | collective-permute-start | bytes 786440 | tf_op jit(solution)/shard_map/ppermute | solution.py:20
  38.5 11.0 %collective-permute-start.2 = (f32[256,256]{1,0:T(8,128)S(1)}, f32[256,256]{1,0:T(8,128)S(1)}, u32[]{:S(2)}, u32[]{:S(2)}) collective-permute-start(f32[256,256]{1,0:T(8,128)S(1)} %get-tuple-element.15), channel_id=1, source_target_pairs={{0,16},{8,24},{16,0},{24,8},{1,17},{9,25},{17,1},{25,9},{2,18},{10... | collective-permute-start | bytes 786440 | tf_op jit(solution)/shard_map/ppermute | solution.py:20
  39.0 12.1 %collective-permute-start.3 = (f32[256,256]{1,0:T(8,128)S(1)}, f32[256,256]{1,0:T(8,128)S(1)}, u32[]{:S(2)}, u32[]{:S(2)}) collective-permute-start(f32[256,256]{1,0:T(8,128)S(1)} %get-tuple-element.16), channel_id=1, source_target_pairs={{0,16},{8,24},{16,0},{24,8},{1,17},{9,25},{17,1},{25,9},{2,18},{10... | collective-permute-start | bytes 786440 | tf_op jit(solution)/shard_map/ppermute | solution.py:20
  47.2 41.4 %copy-start.12 = (s32[8]{0:T(128)S(1)}, s32[8]{0:T(128)}, u32[]{:S(2)}) copy-start(s32[8]{0:T(128)} %param.7) | copy-start | bytes 100
  51.3 1.2 collective-permute-start.6
  52.5 3.6 %collective-permute-start.7 = (f32[256]{0:T(256)S(1)}, f32[256]{0:T(256)S(1)}, u32[]{:S(2)}, u32[]{:S(2)}) collective-permute-start(f32[256]{0:T(256)S(1)} %add.78), channel_id=1, source_target_pairs={{0,2},{1,3},{2,0},{3,1},{4,6},{5,7},{6,4},{7,5},{8,10},{9,11},{10,... | collective-permute-start | bytes 3080 | tf_op jit(solution)/shard_map/ppermute | solution.py:20
  56.1 4.5 %collective-permute-start.8 = (f32[256]{0:T(256)S(1)}, f32[256]{0:T(256)S(1)}, u32[]{:S(2)}, u32[]{:S(2)}) collective-permute-start(f32[256]{0:T(256)S(1)} %add.79), channel_id=1, source_target_pairs={{0,4},{1,5},{2,6},{3,7},{4,0},{5,1},{6,2},{7,3},{8,12},{9,13},{10,... | collective-permute-start | bytes 3080 | tf_op jit(solution)/shard_map/ppermute | solution.py:20
  60.8 29.0 %copy-start.1 = (bf16[256,512]{1,0:T(8,128)(2,1)}, bf16[256,512]{1,0:T(8,128)(2,1)S(1)}, u32[]{:S(2)}) copy-start(bf16[256,512]{1,0:T(8,128)(2,1)S(1)} %get-tuple-element.20.refs_0_) | copy-start | bytes 786436
  60.8 11.0 %collective-permute-start.11 = (bf16[256,512]{1,0:T(8,128)(2,1)S(1)}, bf16[256,512]{1,0:T(8,128)(2,1)S(1)}, u32[]{:S(2)}, u32[]{:S(2)}) collective-permute-start(bf16[256,512]{1,0:T(8,128)(2,1)S(1)} %get-tuple-element.20.refs_0_), channel_id=1, source_target_pairs={{0,6},{1,7},{2,4},{3,5},{4,2},{5,3},{6,0},{7,1},{8,14},{9,15},{10,... | collective-permute-start | bytes 786440 | tf_op jit(solution)/shard_map/ppermute | solution.py:20
  64.4 20.3 %collective-permute-start.10 = (bf16[256,512]{1,0:T(8,128)(2,1)S(1)}, bf16[256,512]{1,0:T(8,128)(2,1)S(1)}, u32[]{:S(2)}, u32[]{:S(2)}) collective-permute-start(bf16[256,512]{1,0:T(8,128)(2,1)S(1)} %get-tuple-element.20.refs_0_), channel_id=1, source_target_pairs={{0,4},{1,5},{2,6},{3,7},{4,0},{5,1},{6,2},{7,3},{8,12},{9,13},{10,... | collective-permute-start | bytes 786440 | tf_op jit(solution)/shard_map/ppermute | solution.py:20
  64.4 20.3 %collective-permute-start.9 = (bf16[256,512]{1,0:T(8,128)(2,1)S(1)}, bf16[256,512]{1,0:T(8,128)(2,1)S(1)}, u32[]{:S(2)}, u32[]{:S(2)}) collective-permute-start(bf16[256,512]{1,0:T(8,128)(2,1)S(1)} %get-tuple-element.20.refs_0_), channel_id=1, source_target_pairs={{0,2},{1,3},{2,0},{3,1},{4,6},{5,7},{6,4},{7,5},{8,10},{9,11},{10,... | collective-permute-start | bytes 786440 | tf_op jit(solution)/shard_map/ppermute | solution.py:20
  65.8 21.3 %collective-permute-start.21 = (bf16[256,512]{1,0:T(8,128)(2,1)S(1)}, bf16[256,512]{1,0:T(8,128)(2,1)S(1)}, u32[]{:S(2)}, u32[]{:S(2)}) collective-permute-start(bf16[256,512]{1,0:T(8,128)(2,1)S(1)} %get-tuple-element.20.refs_0_), channel_id=1, source_target_pairs={{0,24},{8,16},{16,8},{24,0},{1,25},{9,17},{17,9},{25,1},{2,26},{10... | collective-permute-start | bytes 786440 | tf_op jit(solution)/shard_map/ppermute | solution.py:20
  66.1 23.6 %collective-permute-start.20 = (bf16[256,512]{1,0:T(8,128)(2,1)S(1)}, bf16[256,512]{1,0:T(8,128)(2,1)S(1)}, u32[]{:S(2)}, u32[]{:S(2)}) collective-permute-start(bf16[256,512]{1,0:T(8,128)(2,1)S(1)} %get-tuple-element.20.refs_0_), channel_id=1, source_target_pairs={{0,16},{8,24},{16,0},{24,8},{1,17},{9,25},{17,1},{25,9},{2,18},{10... | collective-permute-start | bytes 786440 | tf_op jit(solution)/shard_map/ppermute | solution.py:20
  71.8 17.9 %collective-permute-start.19 = (bf16[256,512]{1,0:T(8,128)(2,1)S(1)}, bf16[256,512]{1,0:T(8,128)(2,1)S(1)}, u32[]{:S(2)}, u32[]{:S(2)}) collective-permute-start(bf16[256,512]{1,0:T(8,128)(2,1)S(1)} %get-tuple-element.20.refs_0_), channel_id=1, source_target_pairs={{0,8},{8,0},{16,24},{24,16},{1,9},{9,1},{17,25},{25,17},{2,10},{10... | collective-permute-start | bytes 786440 | tf_op jit(solution)/shard_map/ppermute | solution.py:20
  85.0 13.9 %copy-start = (bf16[256,512]{1,0:T(8,128)(2,1)}, bf16[256,512]{1,0:T(8,128)(2,1)S(1)}, u32[]{:S(2)}) copy-start(bf16[256,512]{1,0:T(8,128)(2,1)S(1)} %get-tuple-element.10.refs_0_) | copy-start | bytes 786436
  85.0 13.3 %collective-permute-start.17 = (bf16[256,512]{1,0:T(8,128)(2,1)S(1)}, bf16[256,512]{1,0:T(8,128)(2,1)S(1)}, u32[]{:S(2)}, u32[]{:S(2)}) collective-permute-start(bf16[256,512]{1,0:T(8,128)(2,1)S(1)} %get-tuple-element.7), channel_id=1, source_target_pairs={{0,24},{8,16},{16,8},{24,0},{1,25},{9,17},{17,9},{25,1},{2,26},{10... | collective-permute-start | bytes 786440 | tf_op jit(solution)/shard_map/ppermute | solution.py:20
  85.5 12.8 %collective-permute-start.15 = (bf16[256,512]{1,0:T(8,128)(2,1)S(1)}, bf16[256,512]{1,0:T(8,128)(2,1)S(1)}, u32[]{:S(2)}, u32[]{:S(2)}) collective-permute-start(bf16[256,512]{1,0:T(8,128)(2,1)S(1)} %get-tuple-element.8), channel_id=1, source_target_pairs={{0,16},{8,24},{16,0},{24,8},{1,17},{9,25},{17,1},{25,9},{2,18},{10... | collective-permute-start | bytes 786440 | tf_op jit(solution)/shard_map/ppermute | solution.py:20
  87.1 2.7 %copy-start.9 = (bf16[256,512]{1,0:T(8,128)(2,1)}, bf16[256,512]{1,0:T(8,128)(2,1)S(1)}, u32[]{:S(2)}) copy-start(bf16[256,512]{1,0:T(8,128)(2,1)S(1)} %collective-permute-done.21.refs_3_) | copy-start | bytes 786436
  87.1 11.8 %collective-permute-start.13 = (bf16[256,512]{1,0:T(8,128)(2,1)S(1)}, bf16[256,512]{1,0:T(8,128)(2,1)S(1)}, u32[]{:S(2)}, u32[]{:S(2)}) collective-permute-start(bf16[256,512]{1,0:T(8,128)(2,1)S(1)} %get-tuple-element.9), channel_id=1, source_target_pairs={{0,8},{8,0},{16,24},{24,16},{1,9},{9,1},{17,25},{25,17},{2,10},{10... | collective-permute-start | bytes 786440 | tf_op jit(solution)/shard_map/ppermute | solution.py:20
  89.7 0.7 copy-start.10
  89.7 22.0 %collective-permute-start.12 = (bf16[256,512]{1,0:T(8,128)(2,1)S(1)}, bf16[256,512]{1,0:T(8,128)(2,1)S(1)}, u32[]{:S(2)}, u32[]{:S(2)}) collective-permute-start(bf16[256,512]{1,0:T(8,128)(2,1)S(1)} %get-tuple-element.10.refs_0_), channel_id=1, source_target_pairs={{0,1},{1,0},{2,3},{3,2},{4,5},{5,4},{6,7},{7,6},{8,9},{9,8},{10,11... | collective-permute-start | bytes 786440 | tf_op jit(solution)/shard_map/ppermute | solution.py:20
  90.4 0.7 copy-start.11
  98.3 0.7 copy-start.2
  98.3 13.4 %collective-permute-start.18 = (bf16[256,512]{1,0:T(8,128)(2,1)S(1)}, bf16[256,512]{1,0:T(8,128)(2,1)S(1)}, u32[]{:S(2)}, u32[]{:S(2)}) collective-permute-start(bf16[256,512]{1,0:T(8,128)(2,1)S(1)} %collective-permute-done.17.refs_3_), channel_id=1, source_target_pairs={{0,1},{1,0},{2,3},{3,2},{4,5},{5,4},{6,7},{7,6},{8,9},{9,8},{10,11... | collective-permute-start | bytes 786440 | tf_op jit(solution)/shard_map/ppermute | solution.py:20
  98.3 0.8 copy-start.3
  98.3 13.4 %collective-permute-start.16 = (bf16[256,512]{1,0:T(8,128)(2,1)S(1)}, bf16[256,512]{1,0:T(8,128)(2,1)S(1)}, u32[]{:S(2)}, u32[]{:S(2)}) collective-permute-start(bf16[256,512]{1,0:T(8,128)(2,1)S(1)} %collective-permute-done.15.refs_2_), channel_id=1, source_target_pairs={{0,1},{1,0},{2,3},{3,2},{4,5},{5,4},{6,7},{7,6},{8,9},{9,8},{10,11... | collective-permute-start | bytes 786440 | tf_op jit(solution)/shard_map/ppermute | solution.py:20
  98.8 0.7 copy-start.4
  98.8 12.9 %collective-permute-start.14 = (bf16[256,512]{1,0:T(8,128)(2,1)S(1)}, bf16[256,512]{1,0:T(8,128)(2,1)S(1)}, u32[]{:S(2)}, u32[]{:S(2)}) collective-permute-start(bf16[256,512]{1,0:T(8,128)(2,1)S(1)} %collective-permute-done.13.refs_1_), channel_id=1, source_target_pairs={{0,1},{1,0},{2,3},{3,2},{4,5},{5,4},{6,7},{7,6},{8,9},{9,8},{10,11... | collective-permute-start | bytes 786440 | tf_op jit(solution)/shard_map/ppermute | solution.py:20
  111.7 0.7 copy-start.5
  111.7 0.8 copy-start.6
  111.7 0.9 copy-start.7
  111.8 1.0 copy-start.8

commit v2 on v1

v2 whole, which is shorter than its diff:
```python
import functools

import jax
import jax.numpy as jnp
from jax import lax
from jax.experimental import pallas as pl
from jax.experimental.pallas import tpu as pltpu
from jax.sharding import PartitionSpec as P

MAXLAG = 256
LANES = 128
ROWS = 8
GROUP = 16

epsilon = 1e-06


def swap(block, axis, offset):
    size = lax.axis_size(axis)
    return lax.ppermute(block, axis, [(i, i ^ offset) for i in range(size)])


def reorder_chunk(slot, source, ordered, chunk, c):
    blocks = source.shape[0]
    row = lax.broadcasted_iota(jnp.int32, (ROWS, LANES), 0)
    groups = chunk // (3 * GROUP)

    def move(g, carry):
        g = c * groups + g
        base = [slot[g * GROUP + i] for i in range(GROUP)]
        for j in range(blocks):
            tiles = []
            for v in range(3 * GROUP // ROWS):
                tile = None
                for i in range(GROUP):
                    low = 3 * i - ROWS * v
                    if low + 3 <= 0 or low >= ROWS:
                        continue
                    piece = source[j, pl.ds(base[i] + (ROWS - low), ROWS), :]
                    tile = piece if tile is None else jnp.where(row >= low, piece, tile)
                tiles.append(tile)
            ordered[
                pl.ds(pl.multiple_of(g * 3 * GROUP, GROUP), 3 * GROUP), j * LANES : (j + 1) * LANES
            ] = jnp.concatenate(tiles, axis=0).astype(jnp.bfloat16)
        return carry

    lax.fori_loop(0, groups, move, 0, unroll=2)


def write_turned(total, outs):
    half, size = outs[0].shape
    for i in range(len(outs) // 2):
        for h in range(2):
            outs[2 * i + h][...] = total[i * size : (i + 1) * size, h * half : (h + 1) * half].T


def reorder_project_kernel(slot, starts, panel, velocities, *refs, chunk, count):
    outs, ordered_out = refs[: 2 * count], refs[2 * count]
    staged, source, rows, total, in_sems, row_sems, out_sem = refs[2 * count + 1 :]
    depth, width = panel.shape
    blocks = width // LANES
    size = outs[0].shape[1]
    chunks = depth // chunk

    def panel_copy(c):
        part = pl.ds(c * chunk, chunk)
        return pltpu.make_async_copy(panel.at[part, :], staged.at[part, :], in_sems.at[c])

    def row_copy(i):
        first = pl.multiple_of(starts[i], size)
        return pltpu.make_async_copy(
            velocities.at[pl.ds(first, size), :], rows.at[pl.ds(i * size, size), :], row_sems.at[i]
        )

    def ordered_copy(c):
        part = pl.ds(pl.multiple_of(c * chunk, chunk), chunk)
        return pltpu.make_async_copy(staged.at[part, :], ordered_out.at[part, :], out_sem)

    for c in range(chunks):
        panel_copy(c).start()
    for i in range(count):
        row_copy(i).start()
    for c in range(chunks):
        panel_copy(c).wait()

        def widen(i, carry):
            first = pl.multiple_of(c * chunk + i * LANES, LANES)
            for j in range(blocks):
                source[j, pl.ds(ROWS + first, LANES), :] = staged[
                    pl.ds(first, LANES), j * LANES : (j + 1) * LANES
                ].astype(jnp.float32)
            return carry

        lax.fori_loop(0, chunk // LANES, widen, 0)
    for i in range(count):
        row_copy(i).wait()
    total[...] = jnp.zeros_like(total)

    def body(c, carry):
        reorder_chunk(slot, source, staged, chunk, c)
        ordered_copy(c).start()
        part = pl.ds(pl.multiple_of(c * chunk, chunk), chunk)
        total[...] += jnp.dot(rows[:, part], staged[part, :], preferred_element_type=jnp.float32)
        return carry

    lax.fori_loop(0, chunks, body, 0)
    write_turned(total, outs)
    for c in range(chunks):
        ordered_copy(c).wait()


def reorder_project(panel, velocities, slot, starts, size):
    depth, width = panel.shape
    count = starts.shape[0]
    chunk = depth // 10
    anywhere = pl.BlockSpec(memory_space=pl.ANY)
    part = jax.ShapeDtypeStruct((width // 2, size), jnp.float32)
    *parts, ordered = pl.pallas_call(
        functools.partial(reorder_project_kernel, chunk=chunk, count=count),
        out_shape=[part] * (2 * count) + [jax.ShapeDtypeStruct((depth, width), jnp.bfloat16)],
        grid_spec=pltpu.PrefetchScalarGridSpec(
            num_scalar_prefetch=2,
            grid=(1,),
            in_specs=[anywhere] * 2,
            out_specs=[pl.BlockSpec((width // 2, size), lambda i, *_: (0, 0))] * (2 * count) + [anywhere],
            scratch_shapes=[
                pltpu.VMEM((depth, width), jnp.bfloat16),
                pltpu.VMEM((width // LANES, depth + 2 * ROWS, LANES), jnp.float32),
                pltpu.VMEM((count * size, depth), jnp.bfloat16),
                pltpu.VMEM((count * size, width), jnp.float32),
                pltpu.SemaphoreType.DMA((depth // chunk,)),
                pltpu.SemaphoreType.DMA((count,)),
                pltpu.SemaphoreType.DMA,
            ],
        ),
        cost_estimate=pl.CostEstimate(
            flops=2 * count * size * depth * width,
            bytes_accessed=2 * depth * (2 * width + count * size),
            transcendentals=0,
        ),
        name="reorder_project",
    )(slot * 3, starts, panel, velocities)
    return parts, ordered


def project_kernel(starts, panel, velocities, *refs, chunk, count):
    outs = refs[: 2 * count]
    staged, rows, total, sems = refs[2 * count :]
    depth = panel.shape[0]
    size = outs[0].shape[1]
    chunks = depth // chunk

    def copies(c):
        part = pl.ds(c * chunk, chunk)
        yield pltpu.make_async_copy(panel.at[part, :], staged.at[part, :], sems.at[c, count])
        for i in range(count):
            first = pl.multiple_of(starts[i], size)
            yield pltpu.make_async_copy(
                velocities.at[pl.ds(first, size), part], rows.at[pl.ds(i * size, size), part], sems.at[c, i]
            )

    for c in range(chunks):
        for copy in copies(c):
            copy.start()
    for c in range(chunks):
        for copy in copies(c):
            copy.wait()
        part = slice(c * chunk, (c + 1) * chunk)
        product = jnp.dot(rows[:, part], staged[part, :], preferred_element_type=jnp.float32)
        total[...] = product if c == 0 else total[...] + product
    write_turned(total, outs)


def project(ordered, velocities, starts, size):
    depth, width = ordered.shape
    count = starts.shape[0]
    chunk = depth // 5
    anywhere = pl.BlockSpec(memory_space=pl.ANY)
    return pl.pallas_call(
        functools.partial(project_kernel, chunk=chunk, count=count),
        out_shape=[jax.ShapeDtypeStruct((width // 2, size), jnp.float32)] * (2 * count),
        grid_spec=pltpu.PrefetchScalarGridSpec(
            num_scalar_prefetch=1,
            grid=(1,),
            in_specs=[anywhere] * 2,
            out_specs=[pl.BlockSpec((width // 2, size), lambda i, *_: (0, 0))] * (2 * count),
            scratch_shapes=[
                pltpu.VMEM((depth, width), jnp.bfloat16),
                pltpu.VMEM((count * size, depth), jnp.bfloat16),
                pltpu.VMEM((count * size, width), jnp.float32),
                pltpu.SemaphoreType.DMA((depth // chunk, count + 1)),
            ],
        ),
        cost_estimate=pl.CostEstimate(
            flops=2 * count * size * depth * width,
            bytes_accessed=2 * depth * (width + count * size),
            transcendentals=0,
        ),
        name="project",
    )(starts, ordered, velocities)


def shift_kernel(scalars, *refs, parts, lags):
    pieces, out, source = refs[:parts], refs[parts], refs[parts + 1]
    blocks, length, _ = source.shape
    size = pieces[0].shape[1]
    snapshots = parts * size

    @pl.when(pl.program_id(0) == 0)
    def _():
        for j in range(blocks):
            columns = slice(j * LANES, (j + 1) * LANES)
            for m, piece in enumerate(pieces):
                start = pl.multiple_of((scalars[lags] ^ m) * size, size)
                source[j, pl.ds(start, size), :] = piece[columns, :].astype(jnp.float32).T
            source[j, snapshots:, :] = jnp.zeros((length - snapshots, LANES), jnp.float32)

    offset = scalars[pl.program_id(0)]
    step = 128

    def body(i, carry):
        first = pl.multiple_of(i * step, step)
        for j in range(blocks):
            out[0, pl.ds(first, step), j * LANES : (j + 1) * LANES] = source[
                j, pl.ds(first + offset, step), :
            ].astype(jnp.bfloat16)
        return carry

    lax.fori_loop(0, snapshots // step, body, 0)


def shifted_copies(pieces, lag_offsets, mine):
    width, size = pieces[0].shape
    parts = len(pieces)
    snapshots = size * parts
    lags = lag_offsets.shape[0]
    scalars = jnp.concatenate([lag_offsets, mine.astype(jnp.int32)[None]])
    whole = pl.BlockSpec((width, size), lambda l, s: (0, 0))
    return pl.pallas_call(
        functools.partial(shift_kernel, parts=parts, lags=lags),
        out_shape=jax.ShapeDtypeStruct((lags, snapshots, width), jnp.bfloat16),
        grid_spec=pltpu.PrefetchScalarGridSpec(
            num_scalar_prefetch=1,
            grid=(lags,),
            in_specs=[whole] * parts,
            out_specs=pl.BlockSpec((1, snapshots, width), lambda l, s: (l, 0, 0)),
            scratch_shapes=[pltpu.VMEM((width // LANES, snapshots + MAXLAG + ROWS, LANES), jnp.float32)],
        ),
        cost_estimate=pl.CostEstimate(
            flops=0, bytes_accessed=2 * snapshots * width * (lags + 1), transcendentals=0
        ),
        name="shift",
    )(scalars, *pieces)


def correlate_kernel(scalars, factors, *refs, parts, owners, half):
    mine, others = refs[:parts], refs[parts : parts + owners - 1]
    shifted = refs[parts + owners - 1]
    out, turned, lagged, results, in_sems, lag_sems, out_sems = refs[-7:]
    lags = shifted.shape[0]
    modes, size = mine[0].shape
    copies = []
    for m in range(parts):
        place = pl.ds(pl.multiple_of((scalars[0] ^ m) * size, size), size)
        for k in range(owners):
            piece = mine[m] if k == 0 else others[k - 1].at[m]
            copies.append(
                pltpu.make_async_copy(piece, turned.at[pl.ds(k * modes, modes), place], in_sems.at[m, k])
            )
    for copy in copies:
        copy.start()

    def lag_copy(l):
        return pltpu.make_async_copy(shifted.at[l], lagged.at[l], lag_sems.at[l])

    def out_copies(l):
        for k in range(owners):
            first = ((scalars[1] ^ k) * 2 + half) * modes
            yield pltpu.make_async_copy(
                results.at[l, pl.ds(k * modes, modes), :],
                out.at[l, pl.ds(pl.multiple_of(first, modes), modes), :],
                out_sems.at[l, k],
            )

    for l in range(lags):
        lag_copy(l).start()
    for copy in copies:
        copy.wait()

    def body(l, carry):
        lag_copy(l).wait()
        product = jnp.dot(turned[...], lagged[l], preferred_element_type=jnp.float32)
        results[l] = product * factors[l]
        for copy in out_copies(l):
            copy.start()
        return carry

    lax.fori_loop(0, lags, body, 0)
    for l in range(lags):
        for copy in out_copies(l):
            copy.wait()


def correlate(mine, others, shifted, factors, scalars, half, out_shape, previous):
    modes, size = mine[0].shape
    parts, owners = len(mine), len(others) + 1
    lags, snapshots, width = shifted.shape
    operands = [*mine, *others, shifted]
    aliases = {}
    if previous is not None:
        aliases = {len(operands) + 2: 0}
        operands.append(previous)
    anywhere = pl.BlockSpec(memory_space=pl.ANY)
    return pl.pallas_call(
        functools.partial(correlate_kernel, parts=parts, owners=owners, half=half),
        out_shape=jax.ShapeDtypeStruct(out_shape, jnp.float32),
        grid_spec=pltpu.PrefetchScalarGridSpec(
            num_scalar_prefetch=2,
            grid=(1,),
            in_specs=[anywhere] * len(operands),
            out_specs=anywhere,
            scratch_shapes=[
                pltpu.VMEM((owners * modes, snapshots), jnp.bfloat16),
                pltpu.VMEM((lags, snapshots, width), jnp.bfloat16),
                pltpu.VMEM((lags, owners * modes, width), jnp.float32),
                pltpu.SemaphoreType.DMA((parts, owners)),
                pltpu.SemaphoreType.DMA((lags,)),
                pltpu.SemaphoreType.DMA((lags, owners)),
            ],
        ),
        input_output_aliases=aliases,
        cost_estimate=pl.CostEstimate(
            flops=2 * lags * owners * modes * snapshots * width,
            bytes_accessed=lags * width * (2 * snapshots + 4 * owners * modes),
            transcendentals=0,
        ),
        name="correlate",
    )(scalars, factors, *operands)


def reduce_scatter(held, bits):
    live = range(len(held))
    held = list(held)
    for bit in bits:
        for m in reversed(live):
            if m & bit:
                held[m ^ bit] = held[m ^ bit] + swap(held[m], "row", bit)
        live = [m for m in live if not m & bit]
    return held[0]


def local(velocities, modes_panel, atom_slot, lag_offsets):
    ranks = lax.axis_size("row")
    columns = lax.axis_size("col")
    owners = columns // ranks
    mine = lax.axis_index("row")
    group = lax.axis_index("col") // owners
    member = lax.axis_index("col") % owners
    snapshots = velocities.shape[0]
    size = snapshots // ranks
    width = modes_panel.shape[1]
    modes = width * columns

    first = jnp.stack([(mine ^ m) * size for m in reversed(range(ranks))]).astype(jnp.int32)
    near = ranks // 2
    far_parts, ordered = reorder_project(modes_panel, velocities, atom_slot, first[:near], size)
    near_parts = project(ordered, velocities, first[near:], size)
    parts = [*far_parts, *near_parts]
    bits = [1 << b for b in range(ranks.bit_length() - 1)]
    halves = [
        reduce_scatter([parts[2 * (ranks - 1 - m) + h] for m in range(ranks)], bits[::-1] if h else bits)
        for h in range(2)
    ]

    energy = sum(jnp.sum(half * half, axis=0) for half in halves)
    bit = 1
    while bit < columns:
        energy = energy + swap(energy, "col", bit)
        bit *= 2
    scale = lax.rsqrt(energy / modes + epsilon)[None, :]
    halves = [(half * scale).astype(jnp.bfloat16) for half in halves]
    own = jnp.concatenate(halves, axis=0)

    across = [[piece] + [swap(piece, "col", owners * m) for m in range(1, ranks)] for piece in halves]
    column_pieces = [own] + [swap(own, "row", m) for m in range(1, ranks)]
    shifted = shifted_copies(column_pieces, lag_offsets, mine)

    factors = lax.rsqrt((snapshots - lag_offsets).astype(jnp.float32))
    scalars = jnp.stack([mine, member]).astype(jnp.int32)
    out_shape = (lag_offsets.shape[0], width * owners, width)
    result = None
    for h in range(2):
        if h == 1:
            across[h], shifted = lax.optimization_barrier((across[h], shifted))
        stacked = jnp.stack(across[h])
        pieces = []
        for m in range(ranks):
            chosen = lax.dynamic_index_in_dim(stacked, group ^ mine ^ m, 0, keepdims=False)
            pieces.append(chosen if m == 0 else swap(chosen, "row", m))
        if h == 1:
            pieces, result = lax.optimization_barrier((pieces, result))
        joined = jnp.stack(pieces)
        others = [swap(joined, "col", k) for k in range(1, owners)]
        result = correlate(pieces, others, shifted, factors, scalars, h, out_shape, result)
    return result


def solution(mesh):
    return jax.shard_map(
        local,
        mesh=mesh,
        in_specs=(P(None, "row"), P("row", "col"), P("row"), P()),
        out_specs=P(None, "row", "col"),
        check_vma=False,
    )
```

time: 125 us -> 133 us (1.064)
  matrix products: 26.5 us -> 0 us
  Pallas kernels: 43.3 us -> 56.5 us
  starting transfers between devices: 24.1 us -> 33.1 us
  waiting for transfers between devices: 25.4 us -> 32.2 us
  other arithmetic: 2.29 us -> 8.17 us
    dot_general x4 -> x0, matrix products: 26.5 us -> none  [local(): pieces[m] = jnp.dot(rows, panel, preferred_element_type=jnp.float32)]
    pallas_call x3 -> x4, Pallas kernels: 36.1 us -> 49.1 us  [the longest x2 21.8 us: correlate(): pl.pallas_call(functools.partial(correlate_kernel, parts=parts, owners=ow...]
    ppermute x22 -> x26, starting transfers between devices: 24.1 us -> 33.1 us  [swap(): return lax.ppermute(block, axis, [(i, i ^ offset) for i in range(size)])]
    ppermute x22 -> x26, waiting for transfers between devices: 25.4 us -> 32.2 us  [swap(): return lax.ppermute(block, axis, [(i, i ^ offset) for i in range(size)])]
    reduce_sum x1 -> x2, other arithmetic: 0.15 us -> 2.03 us  [local(): energy = sum((jnp.sum(half * half, axis=0) for half in halves))]
    unnamed x26 -> x32, local copies, waits for them, and re-layouts: 2.96 us -> 2.41 us
  transfers between devices with their start and end apart: 22 -> 26, of which waited for: 7 -> 12; matrix products, arithmetic and copies ran while one was open for 18% -> 3% of each run, Pallas kernels for 15% -> 20%
where the time goes in v2:
time: 133 us
  Pallas kernels  56.5 us (42%)
  starting transfers between devices  33.1 us (25%)
  waiting for transfers between devices  32.2 us (24%)
  other arithmetic  8.17 us (6%)
  local copies, waits for them, and re-layouts  2.51 us (2%)
    ppermute x26, starting transfers between devices, swap(): return lax.ppermute(block, axis, [(i, i ^ offset) for i in range(size)])  33.1 us
    ppermute x26, waiting for transfers between devices, swap(): return lax.ppermute(block, axis, [(i, i ^ offset) for i in range(size)])  32.2 us
    pallas_call x2, Pallas kernels, correlate(): pl.pallas_call(functools.partial(correlate_kernel, parts=parts, owners=ow...  21.8 us
    pallas_call x1, Pallas kernels, reorder_project(): pl.pallas_call(functools.partial(reorder_project_kernel, chunk=chunk, cou...  18.9 us
    pallas_call x1, Pallas kernels, project(): pl.pallas_call(functools.partial(project_kernel, chunk=chunk, count=count...  8.41 us
    pallas_call x1, Pallas kernels, shifted_copies(): pl.pallas_call(functools.partial(shift_kernel, parts=parts, lags=lags), o...  7.41 us
  transfers between devices with their start and end apart: 26, of which 12 were waited for; matrix products, arithmetic and copies ran while one was open for 3% of the time, Pallas kernels for 20%

profile of v2, /device:TPU:0, one launch (start us, length us, event | category | flops | bytes accessed | tf_op | source)
XLA Modules:
  0.0 132.8 jit_solution(549008906599404277)
XLA Ops:
  0.0 1.3 broadcast_multiply_fusion.slot
  1.3 0.6 pad_add_fusion.1
  1.9 18.9 %reorder_project.1 = (f32[256,256]{1,0:T(8,128)}, f32[256,256]{1,0:T(8,128)}, f32[256,256]{1,0:T(8,128)}, f32[256,256]{1,0:T(8,128)}, bf16[7680,512]{1,0:T(8,128)(2,1)}) custom-call(s32[2560]{0:T(1024)} %broadcast_multiply_fusion.slot, s32[2]{0:T(128)} %get-tuple-element.54.starts, bf16[7680,512]{1,0:T(8,128)(2,1)} %panel.1, bf16[1024,7680]{1,0:T(8,128)(2,1)} %velocities.3), custom_call_target="tpu_custom_call" | custom-call | flops 4026531840 | bytes 23592960 | tf_op jit(solution)/shard_map/reorder_project/pallas_call | solution.py:118
  20.8 3.0 %collective-permute-start = (f32[256,256]{1,0:T(8,128)}, f32[256,256]{1,0:T(8,128)S(1)}, u32[]{:S(2)}, u32[]{:S(2)}) collective-permute-start(f32[256,256]{1,0:T(8,128)} %get-tuple-element.26), channel_id=1, source_target_pairs={{0,16},{8,24},{16,0},{24,8},{1,17},{9,25},{17,1},{25,9},{2,18},{10... | collective-permute-start | bytes 786440 | tf_op jit(solution)/shard_map/ppermute | solution.py:20
  23.8 0.1 collective-permute-start.1
  23.9 1.9 %collective-permute-start.4 = (f32[256,256]{1,0:T(8,128)}, f32[256,256]{1,0:T(8,128)S(1)}, u32[]{:S(2)}, u32[]{:S(2)}) collective-permute-start(f32[256,256]{1,0:T(8,128)} %get-tuple-element.32), channel_id=1, source_target_pairs={{0,8},{8,0},{16,24},{24,16},{1,9},{9,1},{17,25},{25,17},{2,10},{10... | collective-permute-start | bytes 786440 | tf_op jit(solution)/shard_map/ppermute | solution.py:20
  25.8 8.4 %project.1 = (f32[256,256]{1,0:T(8,128)}, f32[256,256]{1,0:T(8,128)}, f32[256,256]{1,0:T(8,128)}, f32[256,256]{1,0:T(8,128)}) custom-call(s32[2]{0:T(128)} %get-tuple-element.53.starts, bf16[7680,512]{1,0:T(8,128)(2,1)} %get-tuple-element.24.panel, bf16[1024,7680]{1,0:T(8,128)(2,1)} %velocities.3), custom_call_target="tpu_custom_call" | custom-call | flops 4026531840 | bytes 15728640 | tf_op jit(solution)/shard_map/project/pallas_call | solution.py:179
  34.2 1.7 %collective-permute-done.1 = f32[256,256]{1,0:T(8,128)S(1)} collective-permute-done((f32[256,256]{1,0:T(8,128)}, f32[256,256]{1,0:T(8,128)S(1)}, u32[]{:S(2)}, u32[]{:S(2)}) %collective-permute-start.1) | collective-permute-done | bytes 262176 | tf_op jit(solution)/shard_map/ppermute | solution.py:20
  36.0 1.0 add.60
  37.0 1.8 %collective-permute-start.2 = (f32[256,256]{1,0:T(8,128)S(1)}, f32[256,256]{1,0:T(8,128)S(1)}, u32[]{:S(2)}, u32[]{:S(2)}) collective-permute-start(f32[256,256]{1,0:T(8,128)S(1)} %add.60), channel_id=1, source_target_pairs={{0,8},{8,0},{16,24},{24,16},{1,9},{9,1},{17,25},{25,17},{2,10},{10... | collective-permute-start | bytes 786440 | tf_op jit(solution)/shard_map/ppermute | solution.py:20
  38.7 0.3 collective-permute-start.3
  39.1 0.0 collective-permute-done.4
  39.1 1.8 %collective-permute-start.5 = (f32[256,256]{1,0:T(8,128)S(1)}, f32[256,256]{1,0:T(8,128)S(1)}, u32[]{:S(2)}, u32[]{:S(2)}) collective-permute-start(f32[256,256]{1,0:T(8,128)S(1)} %add.63), channel_id=1, source_target_pairs={{0,16},{8,24},{16,0},{24,8},{1,17},{9,25},{17,1},{25,9},{2,18},{10... | collective-permute-start | bytes 786440 | tf_op jit(solution)/shard_map/ppermute | solution.py:20
  40.9 0.0 collective-permute-done
  40.9 5.3 %collective-permute-done.2 = f32[256,256]{1,0:T(8,128)S(1)} collective-permute-done((f32[256,256]{1,0:T(8,128)S(1)}, f32[256,256]{1,0:T(8,128)S(1)}, u32[]{:S(2)}, u32[]{:S(2)}) %collective-permute-start.2) | collective-permute-done | bytes 262176 | tf_op jit(solution)/shard_map/ppermute | solution.py:20
  46.2 1.0 multiply_reduce_fusion
  47.2 2.9 %collective-permute-done.3 = f32[256,256]{1,0:T(8,128)S(1)} collective-permute-done((f32[256,256]{1,0:T(8,128)}, f32[256,256]{1,0:T(8,128)S(1)}, u32[]{:S(2)}, u32[]{:S(2)}) %collective-permute-start.3) | collective-permute-done | bytes 262176 | tf_op jit(solution)/shard_map/ppermute | solution.py:20
  50.1 1.0 multiply_reduce_fusion.1
  51.1 0.1 collective-permute-start.6
  51.2 1.1 collective-permute-done.6
  52.4 1.5 %collective-permute-start.7 = (f32[256]{0:T(256)S(1)}, f32[256]{0:T(256)S(1)}, u32[]{:S(2)}, u32[]{:S(2)}) collective-permute-start(f32[256]{0:T(256)S(1)} %add.66), channel_id=1, source_target_pairs={{0,2},{1,3},{2,0},{3,1},{4,6},{5,7},{6,4},{7,5},{8,10},{9,11},{10,... | collective-permute-start | bytes 3080 | tf_op jit(solution)/shard_map/ppermute | solution.py:20
  53.9 2.0 %collective-permute-done.7 = f32[256]{0:T(256)S(1)} collective-permute-done((f32[256]{0:T(256)S(1)}, f32[256]{0:T(256)S(1)}, u32[]{:S(2)}, u32[]{:S(2)}) %collective-permute-start.7) | collective-permute-done | bytes 1056 | tf_op jit(solution)/shard_map/ppermute | solution.py:20
  55.9 2.6 %collective-permute-start.8 = (f32[256]{0:T(256)S(1)}, f32[256]{0:T(256)S(1)}, u32[]{:S(2)}, u32[]{:S(2)}) collective-permute-start(f32[256]{0:T(256)S(1)} %add.67), channel_id=1, source_target_pairs={{0,4},{1,5},{2,6},{3,7},{4,0},{5,1},{6,2},{7,3},{8,12},{9,13},{10,... | collective-permute-start | bytes 3080 | tf_op jit(solution)/shard_map/ppermute | solution.py:20
  58.5 1.9 %collective-permute-done.8 = f32[256]{0:T(256)S(1)} collective-permute-done((f32[256]{0:T(256)S(1)}, f32[256]{0:T(256)S(1)}, u32[]{:S(2)}, u32[]{:S(2)}) %collective-permute-start.8) | collective-permute-done | bytes 1056 | tf_op jit(solution)/shard_map/ppermute | solution.py:20
  60.4 1.1 multiply_convert_fusion
  61.6 3.6 %collective-permute-start.20 = (bf16[256,256]{1,0:T(8,128)(2,1)S(1)}, bf16[256,256]{1,0:T(8,128)(2,1)S(1)}, u32[]{:S(2)}, u32[]{:S(2)}) collective-permute-start(bf16[256,256]{1,0:T(8,128)(2,1)S(1)} %get-tuple-element.51), channel_id=1, source_target_pairs={{0,6},{1,7},{2,4},{3,5},{4,2},{5,3},{6,0},{7,1},{8,14},{9,15},{10,... | collective-permute-start | bytes 393224 | tf_op jit(solution)/shard_map/ppermute | solution.py:20
  65.2 0.0 collective-permute-start.19
  65.2 0.8 collective-permute-start.18
  66.0 3.3 %collective-permute-done.20 = bf16[256,256]{1,0:T(8,128)(2,1)S(1)} collective-permute-done((bf16[256,256]{1,0:T(8,128)(2,1)S(1)}, bf16[256,256]{1,0:T(8,128)(2,1)S(1)}, u32[]{:S(2)}, u32[]{:S(2)}) %collective-permute-start.20) | collective-permute-done | bytes 131104 | tf_op jit(solution)/shard_map/ppermute | solution.py:20
  69.3 5.0 %collective-permute-done.19 = bf16[256,256]{1,0:T(8,128)(2,1)S(1)} collective-permute-done((bf16[256,256]{1,0:T(8,128)(2,1)S(1)}, bf16[256,256]{1,0:T(8,128)(2,1)S(1)}, u32[]{:S(2)}, u32[]{:S(2)}) %collective-permute-start.19) | collective-permute-done | bytes 131104 | tf_op jit(solution)/shard_map/ppermute | solution.py:20
  74.3 0.0 collective-permute-done.18
  74.3 0.1 pad_maximum_fusion.1
  74.4 2.5 %collective-permute-start.23 = (bf16[256,256]{1,0:T(8,128)(2,1)S(1)}, bf16[256,256]{1,0:T(8,128)(2,1)S(1)}, u32[]{:S(2)}, u32[]{:S(2)}) collective-permute-start(bf16[256,256]{1,0:T(8,128)(2,1)S(1)} %get-tuple-element.43), channel_id=1, source_target_pairs={{0,24},{8,16},{16,8},{24,0},{1,25},{9,17},{17,9},{25,1},{2,26},{10... | collective-permute-start | bytes 393224 | tf_op jit(solution)/shard_map/ppermute | solution.py:20
  77.0 0.4 collective-permute-start.22
  77.4 0.6 collective-permute-start.21
  78.0 0.0 copy-start.2
  78.0 2.5 %collective-permute-start.14 = (bf16[512,256]{1,0:T(8,128)(2,1)S(1)}, bf16[512,256]{1,0:T(8,128)(2,1)S(1)}, u32[]{:S(2)}, u32[]{:S(2)}) collective-permute-start(bf16[512,256]{1,0:T(8,128)(2,1)S(1)} %pad_maximum_fusion.4.refs_0_), channel_id=1, source_target_pairs={{0,24},{8,16},{16,8},{24,0},{1,25},{9,17},{17,9},{25,1},{2,26},{10... | collective-permute-start | bytes 786440 | tf_op jit(solution)/shard_map/ppermute | solution.py:20
  80.6 0.4 collective-permute-start.13
  81.0 0.1 collective-permute-done.23.refs_3_
  81.1 2.1 %collective-permute-start.12 = (bf16[512,256]{1,0:T(8,128)(2,1)S(1)}, bf16[512,256]{1,0:T(8,128)(2,1)S(1)}, u32[]{:S(2)}, u32[]{:S(2)}) collective-permute-start(bf16[512,256]{1,0:T(8,128)(2,1)S(1)} %pad_maximum_fusion.4.refs_0_), channel_id=1, source_target_pairs={{0,8},{8,0},{16,24},{24,16},{1,9},{9,1},{17,25},{25,17},{2,10},{10... | collective-permute-start | bytes 786440 | tf_op jit(solution)/shard_map/ppermute | solution.py:20
  83.2 4.8 %collective-permute-done.22.refs_2_ = bf16[256,256]{1,0:T(8,128)(2,1)S(1)} collective-permute-done((bf16[256,256]{1,0:T(8,128)(2,1)S(1)}, bf16[256,256]{1,0:T(8,128)(2,1)S(1)}, u32[]{:S(2)}, u32[]{:S(2)}) %collective-permute-start.22) | collective-permute-done | bytes 131104 | tf_op jit(solution)/shard_map/ppermute | solution.py:20
  88.1 0.1 pad_maximum_fusion.2
  88.1 0.1 collective-permute-start.24
  88.2 0.5 convert_rsqrt_fusion.factors
  88.8 3.2 %collective-permute-start.11 = (bf16[256,256]{1,0:T(8,128)(2,1)S(1)}, bf16[256,256]{1,0:T(8,128)(2,1)S(1)}, u32[]{:S(2)}, u32[]{:S(2)}) collective-permute-start(bf16[256,256]{1,0:T(8,128)(2,1)S(1)} %get-tuple-element.33), channel_id=1, source_target_pairs={{0,6},{1,7},{2,4},{3,5},{4,2},{5,3},{6,0},{7,1},{8,14},{9,15},{10,... | collective-permute-start | bytes 393224 | tf_op jit(solution)/shard_map/ppermute | solution.py:20
  92.0 0.0 collective-permute-done.14.refs_3_
  92.0 2.0 %collective-permute-done.13.refs_2_ = bf16[512,256]{1,0:T(8,128)(2,1)S(1)} collective-permute-done((bf16[512,256]{1,0:T(8,128)(2,1)S(1)}, bf16[512,256]{1,0:T(8,128)(2,1)S(1)}, u32[]{:S(2)}, u32[]{:S(2)}) %collective-permute-start.13) | collective-permute-done | bytes 262176 | tf_op jit(solution)/shard_map/ppermute | solution.py:20
  94.0 0.6 pad_add_fusion.3.scalars
  94.7 0.6 pad_add_fusion.scalars
  95.2 0.0 collective-permute-done.12.refs_1_
  95.3 0.7 copy-done.13
  96.0 7.4 %shift.1.refs_5_ = bf16[8,1024,512]{2,1,0:T(8,128)(2,1)} custom-call(s32[9]{0:T(128)} %pad_add_fusion.3.scalars, bf16[512,256]{1,0:T(8,128)(2,1)} %copy-done.2, bf16[512,256]{1,0:T(8,128)(2,1)} %copy-done.13, bf16[512,256]{1,0:T(8,128)(2,1)} %copy-done.12, bf16[512,256]{1,0:T(8,128)(2,1)} %copy-done.11), custom_call_target="tpu_custom_call" | custom-call | bytes 9437184 | tf_op jit(solution)/shard_map/shift/pallas_call | solution.py:239
  103.4 0.0 collective-permute-done.11
  103.4 0.1 pad_maximum_fusion
  103.5 1.8 %collective-permute-start.17 = (bf16[256,256]{1,0:T(8,128)(2,1)S(1)}, bf16[256,256]{1,0:T(8,128)(2,1)S(1)}, u32[]{:S(2)}, u32[]{:S(2)}) collective-permute-start(bf16[256,256]{1,0:T(8,128)(2,1)S(1)} %get-tuple-element.47), channel_id=1, source_target_pairs={{0,24},{8,16},{16,8},{24,0},{1,25},{9,17},{17,9},{25,1},{2,26},{10... | collective-permute-start | bytes 393224 | tf_op jit(solution)/shard_map/ppermute | solution.py:20
  105.4 1.2 collective-permute-start.16
  106.5 0.6 collective-permute-start.15
  107.1 0.8 copy-done.10
  108.0 10.9 %correlate.2.refs_6_ = f32[8,1024,512]{2,1,0:T(8,128)} custom-call(s32[2]{0:T(128)} %pad_add_fusion.scalars, f32[8]{0:T(128)} %convert_rsqrt_fusion.factors, bf16[256,256]{1,0:T(8,128)(2,1)} %bitcast.36, bf16[256,256]{1,0:T(8,128)(2,1)} %copy-done.6, bf16[256,256]{1,0:T(8,128)(2,1)} %copy-done.5, bf16[256,256]{1,0:T(8,128)(2,1)} %copy-done.4, ...), custom_call_target="tpu_custom_call" | custom-call | flops 4294967296 | bytes 16777216 | tf_op jit(solution)/shard_map/correlate/pallas_call | solution.py:314
  118.9 0.1 pad_maximum_fusion.3
  119.0 0.1 collective-permute-start.25
  119.1 1.9 %collective-permute-done.25.refs_4_ = bf16[4,256,256]{2,1,0:T(8,128)(2,1)S(1)} collective-permute-done((bf16[4,256,256]{2,1,0:T(8,128)(2,1)S(1)}, bf16[4,256,256]{2,1,0:T(8,128)(2,1)S(1)}, u32[]{:S(2)}, u32[]{:S(2)}) %collective-permute-start.25) | collective-permute-done | bytes 524320 | tf_op jit(solution)/shard_map/ppermute | solution.py:20
  121.0 0.8 copy-done.3
  121.9 10.9 %correlate.3 = f32[8,1024,512]{2,1,0:T(8,128)} custom-call(s32[2]{0:T(128)} %pad_add_fusion.scalars, f32[8]{0:T(128)} %convert_rsqrt_fusion.factors, bf16[256,256]{1,0:T(8,128)(2,1)} %copy-done.1, bf16[256,256]{1,0:T(8,128)(2,1)} %copy-done.9, bf16[256,256]{1,0:T(8,128)(2,1)} %copy-done.8, ...), custom_call_target="tpu_custom_call", output_to_operand_aliasing={{}: (8, {})} | custom-call | flops 4294967296 | bytes 16777216 | tf_op jit(solution)/shard_map/correlate/pallas_call | solution.py:314
  (46 shorter events, 0.2 us)
Async XLA Ops:
  20.8 18.3 %copy-start.14 = (f32[256,256]{1,0:T(8,128)S(1)}, f32[256,256]{1,0:T(8,128)}, u32[]{:S(2)}) copy-start(f32[256,256]{1,0:T(8,128)} %get-tuple-element.31) | copy-start | bytes 786436
  20.8 20.1 %collective-permute-start = (f32[256,256]{1,0:T(8,128)}, f32[256,256]{1,0:T(8,128)S(1)}, u32[]{:S(2)}, u32[]{:S(2)}) collective-permute-start(f32[256,256]{1,0:T(8,128)} %get-tuple-element.26), channel_id=1, source_target_pairs={{0,16},{8,24},{16,0},{24,8},{1,17},{9,25},{17,1},{25,9},{2,18},{10... | collective-permute-start | bytes 786440 | tf_op jit(solution)/shard_map/ppermute | solution.py:20
  23.8 12.1 %collective-permute-start.1 = (f32[256,256]{1,0:T(8,128)}, f32[256,256]{1,0:T(8,128)S(1)}, u32[]{:S(2)}, u32[]{:S(2)}) collective-permute-start(f32[256,256]{1,0:T(8,128)} %get-tuple-element.28), channel_id=1, source_target_pairs={{0,16},{8,24},{16,0},{24,8},{1,17},{9,25},{17,1},{25,9},{2,18},{10... | collective-permute-start | bytes 786440 | tf_op jit(solution)/shard_map/ppermute | solution.py:20
  23.9 15.1 %collective-permute-start.4 = (f32[256,256]{1,0:T(8,128)}, f32[256,256]{1,0:T(8,128)S(1)}, u32[]{:S(2)}, u32[]{:S(2)}) collective-permute-start(f32[256,256]{1,0:T(8,128)} %get-tuple-element.32), channel_id=1, source_target_pairs={{0,8},{8,0},{16,24},{24,16},{1,9},{9,1},{17,25},{25,17},{2,10},{10... | collective-permute-start | bytes 786440 | tf_op jit(solution)/shard_map/ppermute | solution.py:20
  25.8 62.4 %copy-start.15 = (s32[8]{0:T(128)S(1)}, s32[8]{0:T(128)}, u32[]{:S(2)}) copy-start(s32[8]{0:T(128)} %param.7) | copy-start | bytes 100
  37.0 9.2 %collective-permute-start.2 = (f32[256,256]{1,0:T(8,128)S(1)}, f32[256,256]{1,0:T(8,128)S(1)}, u32[]{:S(2)}, u32[]{:S(2)}) collective-permute-start(f32[256,256]{1,0:T(8,128)S(1)} %add.60), channel_id=1, source_target_pairs={{0,8},{8,0},{16,24},{24,16},{1,9},{9,1},{17,25},{25,17},{2,10},{10... | collective-permute-start | bytes 786440 | tf_op jit(solution)/shard_map/ppermute | solution.py:20
  38.7 11.4 %collective-permute-start.3 = (f32[256,256]{1,0:T(8,128)}, f32[256,256]{1,0:T(8,128)S(1)}, u32[]{:S(2)}, u32[]{:S(2)}) collective-permute-start(f32[256,256]{1,0:T(8,128)} %get-tuple-element.30), channel_id=1, source_target_pairs={{0,8},{8,0},{16,24},{24,16},{1,9},{9,1},{17,25},{25,17},{2,10},{10... | collective-permute-start | bytes 786440 | tf_op jit(solution)/shard_map/ppermute | solution.py:20
  39.1 11.0 %collective-permute-start.5 = (f32[256,256]{1,0:T(8,128)S(1)}, f32[256,256]{1,0:T(8,128)S(1)}, u32[]{:S(2)}, u32[]{:S(2)}) collective-permute-start(f32[256,256]{1,0:T(8,128)S(1)} %add.63), channel_id=1, source_target_pairs={{0,16},{8,24},{16,0},{24,8},{1,17},{9,25},{17,1},{25,9},{2,18},{10... | collective-permute-start | bytes 786440 | tf_op jit(solution)/shard_map/ppermute | solution.py:20
  51.1 1.2 collective-permute-start.6
  52.4 3.6 %collective-permute-start.7 = (f32[256]{0:T(256)S(1)}, f32[256]{0:T(256)S(1)}, u32[]{:S(2)}, u32[]{:S(2)}) collective-permute-start(f32[256]{0:T(256)S(1)} %add.66), channel_id=1, source_target_pairs={{0,2},{1,3},{2,0},{3,1},{4,6},{5,7},{6,4},{7,5},{8,10},{9,11},{10,... | collective-permute-start | bytes 3080 | tf_op jit(solution)/shard_map/ppermute | solution.py:20
  55.9 4.5 %collective-permute-start.8 = (f32[256]{0:T(256)S(1)}, f32[256]{0:T(256)S(1)}, u32[]{:S(2)}, u32[]{:S(2)}) collective-permute-start(f32[256]{0:T(256)S(1)} %add.67), channel_id=1, source_target_pairs={{0,4},{1,5},{2,6},{3,7},{4,0},{5,1},{6,2},{7,3},{8,12},{9,13},{10,... | collective-permute-start | bytes 3080 | tf_op jit(solution)/shard_map/ppermute | solution.py:20
  61.6 7.8 %collective-permute-start.20 = (bf16[256,256]{1,0:T(8,128)(2,1)S(1)}, bf16[256,256]{1,0:T(8,128)(2,1)S(1)}, u32[]{:S(2)}, u32[]{:S(2)}) collective-permute-start(bf16[256,256]{1,0:T(8,128)(2,1)S(1)} %get-tuple-element.51), channel_id=1, source_target_pairs={{0,6},{1,7},{2,4},{3,5},{4,2},{5,3},{6,0},{7,1},{8,14},{9,15},{10,... | collective-permute-start | bytes 393224 | tf_op jit(solution)/shard_map/ppermute | solution.py:20
  65.2 9.1 %collective-permute-start.19 = (bf16[256,256]{1,0:T(8,128)(2,1)S(1)}, bf16[256,256]{1,0:T(8,128)(2,1)S(1)}, u32[]{:S(2)}, u32[]{:S(2)}) collective-permute-start(bf16[256,256]{1,0:T(8,128)(2,1)S(1)} %get-tuple-element.51), channel_id=1, source_target_pairs={{0,4},{1,5},{2,6},{3,7},{4,0},{5,1},{6,2},{7,3},{8,12},{9,13},{10,... | collective-permute-start | bytes 393224 | tf_op jit(solution)/shard_map/ppermute | solution.py:20
  65.2 9.1 %collective-permute-start.18 = (bf16[256,256]{1,0:T(8,128)(2,1)S(1)}, bf16[256,256]{1,0:T(8,128)(2,1)S(1)}, u32[]{:S(2)}, u32[]{:S(2)}) collective-permute-start(bf16[256,256]{1,0:T(8,128)(2,1)S(1)} %get-tuple-element.51), channel_id=1, source_target_pairs={{0,2},{1,3},{2,0},{3,1},{4,6},{5,7},{6,4},{7,5},{8,10},{9,11},{10,... | collective-permute-start | bytes 393224 | tf_op jit(solution)/shard_map/ppermute | solution.py:20
  74.4 32.7 %copy-start = (bf16[1,256,256]{2,1,0:T(8,128)(2,1)}, bf16[1,256,256]{2,1,0:T(8,128)(2,1)S(1)}, u32[]{:S(2)}) copy-start(bf16[1,256,256]{2,1,0:T(8,128)(2,1)S(1)} %get-tuple-element.46) | copy-start | bytes 393220
  74.4 6.7 %collective-permute-start.23 = (bf16[256,256]{1,0:T(8,128)(2,1)S(1)}, bf16[256,256]{1,0:T(8,128)(2,1)S(1)}, u32[]{:S(2)}, u32[]{:S(2)}) collective-permute-start(bf16[256,256]{1,0:T(8,128)(2,1)S(1)} %get-tuple-element.43), channel_id=1, source_target_pairs={{0,24},{8,16},{16,8},{24,0},{1,25},{9,17},{17,9},{25,1},{2,26},{10... | collective-permute-start | bytes 393224 | tf_op jit(solution)/shard_map/ppermute | solution.py:20
  77.0 11.1 %collective-permute-start.22 = (bf16[256,256]{1,0:T(8,128)(2,1)S(1)}, bf16[256,256]{1,0:T(8,128)(2,1)S(1)}, u32[]{:S(2)}, u32[]{:S(2)}) collective-permute-start(bf16[256,256]{1,0:T(8,128)(2,1)S(1)} %get-tuple-element.44), channel_id=1, source_target_pairs={{0,16},{8,24},{16,0},{24,8},{1,17},{9,25},{17,1},{25,9},{2,18},{10... | collective-permute-start | bytes 393224 | tf_op jit(solution)/shard_map/ppermute | solution.py:20
  77.4 10.6 %collective-permute-start.21 = (bf16[256,256]{1,0:T(8,128)(2,1)S(1)}, bf16[256,256]{1,0:T(8,128)(2,1)S(1)}, u32[]{:S(2)}, u32[]{:S(2)}) collective-permute-start(bf16[256,256]{1,0:T(8,128)(2,1)S(1)} %get-tuple-element.45), channel_id=1, source_target_pairs={{0,8},{8,0},{16,24},{24,16},{1,9},{9,1},{17,25},{25,17},{2,10},{10... | collective-permute-start | bytes 393224 | tf_op jit(solution)/shard_map/ppermute | solution.py:20
  78.0 17.2 %copy-start.2 = (bf16[512,256]{1,0:T(8,128)(2,1)}, bf16[512,256]{1,0:T(8,128)(2,1)S(1)}, u32[]{:S(2)}) copy-start(bf16[512,256]{1,0:T(8,128)(2,1)S(1)} %pad_maximum_fusion.4.refs_0_) | copy-start | bytes 786436
  78.0 13.9 %collective-permute-start.14 = (bf16[512,256]{1,0:T(8,128)(2,1)S(1)}, bf16[512,256]{1,0:T(8,128)(2,1)S(1)}, u32[]{:S(2)}, u32[]{:S(2)}) collective-permute-start(bf16[512,256]{1,0:T(8,128)(2,1)S(1)} %pad_maximum_fusion.4.refs_0_), channel_id=1, source_target_pairs={{0,24},{8,16},{16,8},{24,0},{1,25},{9,17},{17,9},{25,1},{2,26},{10... | collective-permute-start | bytes 786440 | tf_op jit(solution)/shard_map/ppermute | solution.py:20
  80.6 13.4 %collective-permute-start.13 = (bf16[512,256]{1,0:T(8,128)(2,1)S(1)}, bf16[512,256]{1,0:T(8,128)(2,1)S(1)}, u32[]{:S(2)}, u32[]{:S(2)}) collective-permute-start(bf16[512,256]{1,0:T(8,128)(2,1)S(1)} %pad_maximum_fusion.4.refs_0_), channel_id=1, source_target_pairs={{0,16},{8,24},{16,0},{24,8},{1,17},{9,25},{17,1},{25,9},{2,18},{10... | collective-permute-start | bytes 786440 | tf_op jit(solution)/shard_map/ppermute | solution.py:20
  81.1 26.0 %copy-start.4 = (bf16[256,256]{1,0:T(8,128)(2,1)}, bf16[256,256]{1,0:T(8,128)(2,1)S(1)}, u32[]{:S(2)}) copy-start(bf16[256,256]{1,0:T(8,128)(2,1)S(1)} %collective-permute-done.23.refs_3_) | copy-start | bytes 393220
  81.1 14.1 %collective-permute-start.12 = (bf16[512,256]{1,0:T(8,128)(2,1)S(1)}, bf16[512,256]{1,0:T(8,128)(2,1)S(1)}, u32[]{:S(2)}, u32[]{:S(2)}) collective-permute-start(bf16[512,256]{1,0:T(8,128)(2,1)S(1)} %pad_maximum_fusion.4.refs_0_), channel_id=1, source_target_pairs={{0,8},{8,0},{16,24},{24,16},{1,9},{9,1},{17,25},{25,17},{2,10},{10... | collective-permute-start | bytes 786440 | tf_op jit(solution)/shard_map/ppermute | solution.py:20
  88.1 19.1 %copy-start.5 = (bf16[256,256]{1,0:T(8,128)(2,1)}, bf16[256,256]{1,0:T(8,128)(2,1)S(1)}, u32[]{:S(2)}) copy-start(bf16[256,256]{1,0:T(8,128)(2,1)S(1)} %collective-permute-done.22.refs_2_) | copy-start | bytes 393220
  88.1 19.1 %copy-start.6 = (bf16[256,256]{1,0:T(8,128)(2,1)}, bf16[256,256]{1,0:T(8,128)(2,1)S(1)}, u32[]{:S(2)}) copy-start(bf16[256,256]{1,0:T(8,128)(2,1)S(1)} %collective-permute-done.21.refs_1_) | copy-start | bytes 393220
  88.1 19.0 %collective-permute-start.24 = (bf16[4,256,256]{2,1,0:T(8,128)(2,1)S(1)}, bf16[4,256,256]{2,1,0:T(8,128)(2,1)S(1)}, u32[]{:S(2)}, u32[]{:S(2)}) collective-permute-start(bf16[4,256,256]{2,1,0:T(8,128)(2,1)S(1)} %pad_maximum_fusion.2), channel_id=1, source_target_pairs={{0,1},{1,0},{2,3},{3,2},{4,5},{5,4},{6,7},{7,6},{8,9},{9,8},{10,11... | collective-permute-start | bytes 1572872 | tf_op jit(solution)/shard_map/ppermute | solution.py:20
  88.8 14.6 %collective-permute-start.11 = (bf16[256,256]{1,0:T(8,128)(2,1)S(1)}, bf16[256,256]{1,0:T(8,128)(2,1)S(1)}, u32[]{:S(2)}, u32[]{:S(2)}) collective-permute-start(bf16[256,256]{1,0:T(8,128)(2,1)S(1)} %get-tuple-element.33), channel_id=1, source_target_pairs={{0,6},{1,7},{2,4},{3,5},{4,2},{5,3},{6,0},{7,1},{8,14},{9,15},{10,... | collective-permute-start | bytes 393224 | tf_op jit(solution)/shard_map/ppermute | solution.py:20
  92.0 3.3 %copy-start.11 = (bf16[512,256]{1,0:T(8,128)(2,1)}, bf16[512,256]{1,0:T(8,128)(2,1)S(1)}, u32[]{:S(2)}) copy-start(bf16[512,256]{1,0:T(8,128)(2,1)S(1)} %collective-permute-done.14.refs_3_) | copy-start | bytes 786436
  92.0 11.4 %collective-permute-start.10 = (bf16[256,256]{1,0:T(8,128)(2,1)S(1)}, bf16[256,256]{1,0:T(8,128)(2,1)S(1)}, u32[]{:S(2)}, u32[]{:S(2)}) collective-permute-start(bf16[256,256]{1,0:T(8,128)(2,1)S(1)} %get-tuple-element.33), channel_id=1, source_target_pairs={{0,4},{1,5},{2,6},{3,7},{4,0},{5,1},{6,2},{7,3},{8,12},{9,13},{10,... | collective-permute-start | bytes 393224 | tf_op jit(solution)/shard_map/ppermute | solution.py:20
  94.0 1.2 copy-start.12
  94.0 9.4 %collective-permute-start.9 = (bf16[256,256]{1,0:T(8,128)(2,1)S(1)}, bf16[256,256]{1,0:T(8,128)(2,1)S(1)}, u32[]{:S(2)}, u32[]{:S(2)}) collective-permute-start(bf16[256,256]{1,0:T(8,128)(2,1)S(1)} %get-tuple-element.33), channel_id=1, source_target_pairs={{0,2},{1,3},{2,0},{3,1},{4,6},{5,7},{6,4},{7,5},{8,10},{9,11},{10,... | collective-permute-start | bytes 393224 | tf_op jit(solution)/shard_map/ppermute | solution.py:20
  95.3 0.7 copy-start.13
  103.5 17.5 %copy-start.1 = (bf16[256,256]{1,0:T(8,128)(2,1)}, bf16[256,256]{1,0:T(8,128)(2,1)S(1)}, u32[]{:S(2)}) copy-start(bf16[256,256]{1,0:T(8,128)(2,1)S(1)} %get-tuple-element.37.refs_0_) | copy-start | bytes 393220
  103.5 15.3 %collective-permute-start.17 = (bf16[256,256]{1,0:T(8,128)(2,1)S(1)}, bf16[256,256]{1,0:T(8,128)(2,1)S(1)}, u32[]{:S(2)}, u32[]{:S(2)}) collective-permute-start(bf16[256,256]{1,0:T(8,128)(2,1)S(1)} %get-tuple-element.47), channel_id=1, source_target_pairs={{0,24},{8,16},{16,8},{24,0},{1,25},{9,17},{17,9},{25,1},{2,26},{10... | collective-permute-start | bytes 393224 | tf_op jit(solution)/shard_map/ppermute | solution.py:20
  105.4 13.6 %collective-permute-start.16 = (bf16[256,256]{1,0:T(8,128)(2,1)S(1)}, bf16[256,256]{1,0:T(8,128)(2,1)S(1)}, u32[]{:S(2)}, u32[]{:S(2)}) collective-permute-start(bf16[256,256]{1,0:T(8,128)(2,1)S(1)} %get-tuple-element.48), channel_id=1, source_target_pairs={{0,16},{8,24},{16,0},{24,8},{1,17},{9,25},{17,1},{25,9},{2,18},{10... | collective-permute-start | bytes 393224 | tf_op jit(solution)/shard_map/ppermute | solution.py:20
  106.5 12.4 %collective-permute-start.15 = (bf16[256,256]{1,0:T(8,128)(2,1)S(1)}, bf16[256,256]{1,0:T(8,128)(2,1)S(1)}, u32[]{:S(2)}, u32[]{:S(2)}) collective-permute-start(bf16[256,256]{1,0:T(8,128)(2,1)S(1)} %get-tuple-element.49), channel_id=1, source_target_pairs={{0,8},{8,0},{16,24},{24,16},{1,9},{9,1},{17,25},{25,17},{2,10},{10... | collective-permute-start | bytes 393224 | tf_op jit(solution)/shard_map/ppermute | solution.py:20
  107.1 0.9 copy-start.10
  118.9 2.1 %copy-start.7 = (bf16[256,256]{1,0:T(8,128)(2,1)}, bf16[256,256]{1,0:T(8,128)(2,1)S(1)}, u32[]{:S(2)}) copy-start(bf16[256,256]{1,0:T(8,128)(2,1)S(1)} %collective-permute-done.17.refs_3_) | copy-start | bytes 393220
  118.9 2.1 %copy-start.8 = (bf16[256,256]{1,0:T(8,128)(2,1)}, bf16[256,256]{1,0:T(8,128)(2,1)S(1)}, u32[]{:S(2)}) copy-start(bf16[256,256]{1,0:T(8,128)(2,1)S(1)} %collective-permute-done.16.refs_2_) | copy-start | bytes 393220
  118.9 2.1 %copy-start.9 = (bf16[256,256]{1,0:T(8,128)(2,1)}, bf16[256,256]{1,0:T(8,128)(2,1)S(1)}, u32[]{:S(2)}) copy-start(bf16[256,256]{1,0:T(8,128)(2,1)S(1)} %collective-permute-done.15.refs_1_) | copy-start | bytes 393220
  119.0 2.0 %collective-permute-start.25 = (bf16[4,256,256]{2,1,0:T(8,128)(2,1)S(1)}, bf16[4,256,256]{2,1,0:T(8,128)(2,1)S(1)}, u32[]{:S(2)}, u32[]{:S(2)}) collective-permute-start(bf16[4,256,256]{2,1,0:T(8,128)(2,1)S(1)} %pad_maximum_fusion.3), channel_id=1, source_target_pairs={{0,1},{1,0},{2,3},{3,2},{4,5},{5,4},{6,7},{7,6},{8,9},{9,8},{10,11... | collective-permute-start | bytes 1572872 | tf_op jit(solution)/shard_map/ppermute | solution.py:20
  121.0 0.9 copy-start.3
